TPU v7x, 512 devices: a whole 4x4x16 slice. The times are simulated.
512 devices in a mesh: chan: 64 (over x, z_lo, core), seg: 8 (over z_hi, y).
Axes of the slice: x: 4, y: 4, z: 16 (z_hi: 2, z_lo: 8; z = z_hi * 8 + z_lo), core: 2. Of those that a mesh axis runs over, the one named last changes fastest.
Arguments:
- raw_strain: bfloat16 [1024, 2048], P('chan', 'seg'), may hold values from -6 to 6
- w_first: bfloat16 [9, 64], replicated, may hold values from -2 to 2
- w_mid: bfloat16 [1, 9, 64, 64], replicated, may hold values from -0.375 to 0.375
- w_last: bfloat16 [9, 64], replicated, may hold values from -0.375 to 0.375
- lower_src: int32 [64], P('chan'), may hold values from 0 to 63, as said below
- upper_src: int32 [64], P('chan'), may hold values from 0 to 63, as said below
- valid_count: int32 [64], P('chan'), may hold values from 8 to 16, as said below
Outputs:
- stacked: float32 [1024, 33, 1024], P('chan', None, 'seg')
Inputs may be any that keep to these rules, and one draw needn't show every extreme that they name: Taken in the order of the fibre, the blocks form one closed loop through all blocks: upper_src[lower_src[i]] = i, and no block is its own neighbour. The other neighbour in the same closed loop: lower_src[upper_src[i]] = i. The live channels of a block are its first valid_count channels; some block is fully live.
All inputs are finite; a program needn't handle non-finite values.
Results may differ from a plain program's by a relative error of at most 0.0073.
Values may be sent and summed in bfloat16 or wider, within the bound.
A program may use at most 64 MiB of HBM per device.

v0:
```python
import math

import jax
import jax.numpy as jnp
from jax import lax
from jax.sharding import PartitionSpec as P

WIN = 256
NLAG = 64
LAYERS = 3
KER = 3
BAND = 4
F = 128


top_precision = lax.Precision.HIGHEST


def from_behind(shard, axis, by):
    count = lax.axis_size(axis)
    return lax.ppermute(shard, axis, [(i, (i + by) % count) for i in range(count)])


def with_halo(block, sides, width):
    for axis, dim in sides:
        count = lax.axis_size(axis)
        forward = [(i, i + 1) for i in range(count - 1)]
        backward = [(target, source) for source, target in forward]
        low = lax.ppermute(
            lax.slice_in_dim(block, block.shape[dim] - width, None, axis=dim), axis, forward
        )
        high = lax.ppermute(lax.slice_in_dim(block, 0, width, axis=dim), axis, backward)
        block = jnp.concatenate([low, block, high], axis=dim)
    return block


def conv_layer(feature, weight):
    out_rows = feature.shape[1] - KER + 1
    out_cols = feature.shape[2] - KER + 1
    acc_sum = None
    for tap_row in range(KER):
        shifted = jnp.concatenate(
            [
                feature[:, tap_row : tap_row + out_rows, tap_col : tap_col + out_cols]
                for tap_col in range(KER)
            ],
            axis=0,
        )
        tap_weights = weight[tap_row * KER : (tap_row + 1) * KER].reshape(
            KER * feature.shape[0], weight.shape[2]
        )
        tap_sum = jnp.einsum(
            "io,irl->orl", tap_weights, shifted, preferred_element_type=jnp.float32
        )
        acc_sum = tap_sum if acc_sum is None else acc_sum + tap_sum
    return acc_sum


def denoise(extended, w_first, w_mid, w_last):
    hidden = jnp.maximum(conv_layer(extended[None], w_first[:, None, :]), 0.0).astype(jnp.bfloat16)
    hidden = jnp.maximum(conv_layer(hidden, w_mid[0]), 0.0).astype(jnp.bfloat16)
    return conv_layer(hidden, w_last[:, :, None])[0]


def cleaned(masked, noise_est, live_mask, live_total):
    clean_rows = (masked.astype(jnp.float32) - noise_est) * live_mask
    common = jnp.sum(clean_rows, axis=0, keepdims=True) / live_total
    return (clean_rows - common) * live_mask


def dft_tables(width, bins):
    time_ids = jnp.arange(width, dtype=jnp.int32)
    freq_ids = jnp.arange(bins, dtype=jnp.int32)
    phases = time_ids[:, None] * freq_ids[None, :] % width
    angles = phases.astype(jnp.float32) * (2.0 * math.pi / width)
    return (jnp.cos(angles), -jnp.sin(angles))


def band_table(bins):
    bin_ids = jnp.arange(bins, dtype=jnp.int32)
    near_bins = jnp.abs(bin_ids[:, None] - bin_ids[None, :]) <= BAND
    return near_bins.astype(jnp.float32) / (2 * BAND + 1)


def lag_table(width, bins, lags, lag_scale):
    freq_ids = jnp.arange(bins, dtype=jnp.int32)
    shifts = jnp.arange(lags, dtype=jnp.int32) - lags // 2
    phases = jnp.remainder(freq_ids[:, None] * shifts[None, :], width)
    angles = phases.astype(jnp.float32) * (2.0 * math.pi / width)
    gains = jnp.where(freq_ids == 0, 1.0, 2.0).astype(jnp.float32)[:, None] * lag_scale
    return jnp.concatenate([gains * jnp.cos(angles), -gains * jnp.sin(angles)], axis=0)


def whiten(frames, width, bins):
    cos_table, sin_table = dft_tables(width, bins)
    real_part = jnp.dot(frames, cos_table, precision=top_precision)
    imag_part = jnp.dot(frames, sin_table, precision=top_precision)
    power_bins = real_part * real_part + imag_part * imag_part
    smooth = jnp.dot(power_bins, band_table(bins), precision=top_precision)
    mean_power = jnp.mean(power_bins, axis=1, keepdims=True)
    divisor = jnp.sqrt(smooth + 0.1 * mean_power + 1e-06)
    return ((real_part / divisor).astype(jnp.bfloat16), (imag_part / divisor).astype(jnp.bfloat16))


def correlate(own_spec, partner, lag_weights):
    chan_rows = own_spec.shape[1]
    products = jnp.einsum("pasf,qbsf->paqbf", own_spec, partner, preferred_element_type=jnp.float32)
    real_sum = products[0, :, 0] + products[1, :, 1]
    imag_sum = products[1, :, 0] - products[0, :, 1]
    stacked_parts = jnp.concatenate([real_sum, imag_sum], axis=2)
    lagged = jnp.dot(
        stacked_parts.reshape(-1, stacked_parts.shape[2]), lag_weights, precision=top_precision
    )
    return lagged.reshape(chan_rows, -1)


def step_ahead(partner):
    return from_behind(partner, "chan", -1)


def body(raw_strain, w_first, w_mid, w_last, lower_src, upper_src, valid_count):
    chan_rows = raw_strain.shape[0]
    halo_depth = LAYERS
    live_mask = (jnp.arange(chan_rows, dtype=jnp.int32)[:, None] < valid_count[0]).astype(
        jnp.bfloat16
    )
    masked = raw_strain * live_mask
    time_ext = with_halo(masked, (("seg", 1),), halo_depth)
    strips = jnp.stack([time_ext[:halo_depth], time_ext[chan_rows - halo_depth :]])
    all_strips = lax.all_gather(strips[None], "chan", axis=0, tiled=True)
    lower_rows = lax.dynamic_index_in_dim(all_strips, lower_src[0], 0, keepdims=False)[1]
    upper_rows = lax.dynamic_index_in_dim(all_strips, upper_src[0], 0, keepdims=False)[0]
    extended = jnp.concatenate([lower_rows, time_ext, upper_rows], axis=0)
    noise_est = denoise(extended, w_first, w_mid, w_last)
    detrended = cleaned(
        masked, noise_est, live_mask.astype(jnp.float32), valid_count[0].astype(jnp.float32)
    )
    seg_count = detrended.shape[1] // WIN
    real_part, imag_part = whiten(detrended, WIN, F)
    own_spec = jnp.stack(
        [real_part.reshape(chan_rows, seg_count, F), imag_part.reshape(chan_rows, seg_count, F)]
    )
    blocks_total = lax.axis_size("chan")
    offsets = blocks_total // 2 + 1
    lag_weights = lag_table(WIN, F, NLAG, 1.0 / math.sqrt(seg_count * lax.axis_size("seg") * F))
    out_width = chan_rows * NLAG
    results = jnp.zeros((chan_rows, offsets, out_width), jnp.float32)

    def store_block(results, partner, offset):
        corr_block = correlate(own_spec, partner, lag_weights)
        return lax.dynamic_update_slice_in_dim(results, corr_block[:, None], offset, 1)

    results = store_block(results, own_spec, 0)

    def one_turn(offset, carry):
        results, partner = carry
        partner = step_ahead(partner)
        return (store_block(results, partner, offset), partner)

    results, partner = lax.fori_loop(1, offsets, one_turn, (results, own_spec))
    results = lax.psum_scatter(results, "seg", scatter_dimension=2, tiled=True)
    return results


def solution(mesh):
    return jax.shard_map(
        body,
        mesh=mesh,
        in_specs=(P("chan", "seg"), P(), P(), P(), P("chan"), P("chan"), P("chan")),
        out_specs=P("chan", None, "seg"),
        check_vma=False,
    )
```

profile of v0, /device:TPU:1, one launch (start us, length us, event | category | flops | bytes accessed | tf_op | source)
XLA Modules:
  0.0 773.5 jit_solution(1925889930514405871)
XLA Ops:
  17.1 128.6 %all-gather = bf16[128,3,262]{2,1,0:T(4,128)(2,1)S(1)} all-gather(bf16[2,3,262]{2,1,0:T(4,128)(2,1)S(1)} %pad_maximum_fusion.2), channel_id=2, replica_groups=mesh['chan'=64,'seg'=8] {'chan'}, dimensions={0}, use_global_device_ids=true | all-gather | bytes 204360 | tf_op jit(solution)/shard_map/all_gather | solution.py:130
  158.3 436.5 %while.17 = (s32[]{:T(128)}, f32[16,33,1024]{2,0,1:T(8,128)S(1)}, bf16[2,16,1,128]{3,1,0,2:T(8,128)(2,1)S(1)}, bf16[2,16,1,128]{3,1,0,2:T(8,128)(2,1)S(1)}, f32[...) while((s32[]{:T(128)}, f32[16,33,1024]{2,0,1:T(8,128)S(1)}, ...), condition=%wide.region_3.4_spmd, body=%wide.region_2.3_spmd.sunk | while | flops 50601984 | bytes 2097323 | solution.py:160
  180.0 12.9 %collective-permute-start = (bf16[2,16,1,128]{3,1,0,2:T(8,128)(2,1)S(1)}, bf16[2,16,1,128]{3,1,0,2:T(8,128)(2,1)S(1)}, u32[]{:S(2)}, u32[]{:S(2)}) collective-permute-start(bf16[2,16,1,128]{3,1,0,2:T(8,128)(2,1)S(1)} %get-tuple-element.265), channel_id=1, source_target_pairs={{0,504},{8,0},{16,8},{24,16},{32,24},{40,32},{48,40},{56,48},{64,5... | collective-permute-start | bytes 24584 | tf_op jit(solution)/shard_map/while/body/eval_jaxpr/ppermute | solution.py:21
  194.3 12.9 %collective-permute-start = (bf16[2,16,1,128]{3,1,0,2:T(8,128)(2,1)S(1)}, bf16[2,16,1,128]{3,1,0,2:T(8,128)(2,1)S(1)}, u32[]{:S(2)}, u32[]{:S(2)}) collective-permute-start(bf16[2,16,1,128]{3,1,0,2:T(8,128)(2,1)S(1)} %get-tuple-element.265), channel_id=1, source_target_pairs={{0,504},{8,0},{16,8},{24,16},{32,24},{40,32},{48,40},{56,48},{64,5... | collective-permute-start | bytes 24584 | tf_op jit(solution)/shard_map/while/body/eval_jaxpr/ppermute | solution.py:21
  208.6 12.9 %collective-permute-start = (bf16[2,16,1,128]{3,1,0,2:T(8,128)(2,1)S(1)}, bf16[2,16,1,128]{3,1,0,2:T(8,128)(2,1)S(1)}, u32[]{:S(2)}, u32[]{:S(2)}) collective-permute-start(bf16[2,16,1,128]{3,1,0,2:T(8,128)(2,1)S(1)} %get-tuple-element.265), channel_id=1, source_target_pairs={{0,504},{8,0},{16,8},{24,16},{32,24},{40,32},{48,40},{56,48},{64,5... | collective-permute-start | bytes 24584 | tf_op jit(solution)/shard_map/while/body/eval_jaxpr/ppermute | solution.py:21
  237.2 12.9 %collective-permute-start = (bf16[2,16,1,128]{3,1,0,2:T(8,128)(2,1)S(1)}, bf16[2,16,1,128]{3,1,0,2:T(8,128)(2,1)S(1)}, u32[]{:S(2)}, u32[]{:S(2)}) collective-permute-start(bf16[2,16,1,128]{3,1,0,2:T(8,128)(2,1)S(1)} %get-tuple-element.265), channel_id=1, source_target_pairs={{0,504},{8,0},{16,8},{24,16},{32,24},{40,32},{48,40},{56,48},{64,5... | collective-permute-start | bytes 24584 | tf_op jit(solution)/shard_map/while/body/eval_jaxpr/ppermute | solution.py:21
  251.5 12.9 %collective-permute-start = (bf16[2,16,1,128]{3,1,0,2:T(8,128)(2,1)S(1)}, bf16[2,16,1,128]{3,1,0,2:T(8,128)(2,1)S(1)}, u32[]{:S(2)}, u32[]{:S(2)}) collective-permute-start(bf16[2,16,1,128]{3,1,0,2:T(8,128)(2,1)S(1)} %get-tuple-element.265), channel_id=1, source_target_pairs={{0,504},{8,0},{16,8},{24,16},{32,24},{40,32},{48,40},{56,48},{64,5... | collective-permute-start | bytes 24584 | tf_op jit(solution)/shard_map/while/body/eval_jaxpr/ppermute | solution.py:21
  265.8 12.9 %collective-permute-start = (bf16[2,16,1,128]{3,1,0,2:T(8,128)(2,1)S(1)}, bf16[2,16,1,128]{3,1,0,2:T(8,128)(2,1)S(1)}, u32[]{:S(2)}, u32[]{:S(2)}) collective-permute-start(bf16[2,16,1,128]{3,1,0,2:T(8,128)(2,1)S(1)} %get-tuple-element.265), channel_id=1, source_target_pairs={{0,504},{8,0},{16,8},{24,16},{32,24},{40,32},{48,40},{56,48},{64,5... | collective-permute-start | bytes 24584 | tf_op jit(solution)/shard_map/while/body/eval_jaxpr/ppermute | solution.py:21
  280.1 12.9 %collective-permute-start = (bf16[2,16,1,128]{3,1,0,2:T(8,128)(2,1)S(1)}, bf16[2,16,1,128]{3,1,0,2:T(8,128)(2,1)S(1)}, u32[]{:S(2)}, u32[]{:S(2)}) collective-permute-start(bf16[2,16,1,128]{3,1,0,2:T(8,128)(2,1)S(1)} %get-tuple-element.265), channel_id=1, source_target_pairs={{0,504},{8,0},{16,8},{24,16},{32,24},{40,32},{48,40},{56,48},{64,5... | collective-permute-start | bytes 24584 | tf_op jit(solution)/shard_map/while/body/eval_jaxpr/ppermute | solution.py:21
  294.4 12.9 %collective-permute-start = (bf16[2,16,1,128]{3,1,0,2:T(8,128)(2,1)S(1)}, bf16[2,16,1,128]{3,1,0,2:T(8,128)(2,1)S(1)}, u32[]{:S(2)}, u32[]{:S(2)}) collective-permute-start(bf16[2,16,1,128]{3,1,0,2:T(8,128)(2,1)S(1)} %get-tuple-element.265), channel_id=1, source_target_pairs={{0,504},{8,0},{16,8},{24,16},{32,24},{40,32},{48,40},{56,48},{64,5... | collective-permute-start | bytes 24584 | tf_op jit(solution)/shard_map/while/body/eval_jaxpr/ppermute | solution.py:21
  323.1 12.9 %collective-permute-start = (bf16[2,16,1,128]{3,1,0,2:T(8,128)(2,1)S(1)}, bf16[2,16,1,128]{3,1,0,2:T(8,128)(2,1)S(1)}, u32[]{:S(2)}, u32[]{:S(2)}) collective-permute-start(bf16[2,16,1,128]{3,1,0,2:T(8,128)(2,1)S(1)} %get-tuple-element.265), channel_id=1, source_target_pairs={{0,504},{8,0},{16,8},{24,16},{32,24},{40,32},{48,40},{56,48},{64,5... | collective-permute-start | bytes 24584 | tf_op jit(solution)/shard_map/while/body/eval_jaxpr/ppermute | solution.py:21
  337.4 12.9 %collective-permute-start = (bf16[2,16,1,128]{3,1,0,2:T(8,128)(2,1)S(1)}, bf16[2,16,1,128]{3,1,0,2:T(8,128)(2,1)S(1)}, u32[]{:S(2)}, u32[]{:S(2)}) collective-permute-start(bf16[2,16,1,128]{3,1,0,2:T(8,128)(2,1)S(1)} %get-tuple-element.265), channel_id=1, source_target_pairs={{0,504},{8,0},{16,8},{24,16},{32,24},{40,32},{48,40},{56,48},{64,5... | collective-permute-start | bytes 24584 | tf_op jit(solution)/shard_map/while/body/eval_jaxpr/ppermute | solution.py:21
  366.0 12.9 %collective-permute-start = (bf16[2,16,1,128]{3,1,0,2:T(8,128)(2,1)S(1)}, bf16[2,16,1,128]{3,1,0,2:T(8,128)(2,1)S(1)}, u32[]{:S(2)}, u32[]{:S(2)}) collective-permute-start(bf16[2,16,1,128]{3,1,0,2:T(8,128)(2,1)S(1)} %get-tuple-element.265), channel_id=1, source_target_pairs={{0,504},{8,0},{16,8},{24,16},{32,24},{40,32},{48,40},{56,48},{64,5... | collective-permute-start | bytes 24584 | tf_op jit(solution)/shard_map/while/body/eval_jaxpr/ppermute | solution.py:21
  380.3 12.9 %collective-permute-start = (bf16[2,16,1,128]{3,1,0,2:T(8,128)(2,1)S(1)}, bf16[2,16,1,128]{3,1,0,2:T(8,128)(2,1)S(1)}, u32[]{:S(2)}, u32[]{:S(2)}) collective-permute-start(bf16[2,16,1,128]{3,1,0,2:T(8,128)(2,1)S(1)} %get-tuple-element.265), channel_id=1, source_target_pairs={{0,504},{8,0},{16,8},{24,16},{32,24},{40,32},{48,40},{56,48},{64,5... | collective-permute-start | bytes 24584 | tf_op jit(solution)/shard_map/while/body/eval_jaxpr/ppermute | solution.py:21
  408.9 12.9 %collective-permute-start = (bf16[2,16,1,128]{3,1,0,2:T(8,128)(2,1)S(1)}, bf16[2,16,1,128]{3,1,0,2:T(8,128)(2,1)S(1)}, u32[]{:S(2)}, u32[]{:S(2)}) collective-permute-start(bf16[2,16,1,128]{3,1,0,2:T(8,128)(2,1)S(1)} %get-tuple-element.265), channel_id=1, source_target_pairs={{0,504},{8,0},{16,8},{24,16},{32,24},{40,32},{48,40},{56,48},{64,5... | collective-permute-start | bytes 24584 | tf_op jit(solution)/shard_map/while/body/eval_jaxpr/ppermute | solution.py:21
  423.2 12.9 %collective-permute-start = (bf16[2,16,1,128]{3,1,0,2:T(8,128)(2,1)S(1)}, bf16[2,16,1,128]{3,1,0,2:T(8,128)(2,1)S(1)}, u32[]{:S(2)}, u32[]{:S(2)}) collective-permute-start(bf16[2,16,1,128]{3,1,0,2:T(8,128)(2,1)S(1)} %get-tuple-element.265), channel_id=1, source_target_pairs={{0,504},{8,0},{16,8},{24,16},{32,24},{40,32},{48,40},{56,48},{64,5... | collective-permute-start | bytes 24584 | tf_op jit(solution)/shard_map/while/body/eval_jaxpr/ppermute | solution.py:21
  451.8 12.9 %collective-permute-start = (bf16[2,16,1,128]{3,1,0,2:T(8,128)(2,1)S(1)}, bf16[2,16,1,128]{3,1,0,2:T(8,128)(2,1)S(1)}, u32[]{:S(2)}, u32[]{:S(2)}) collective-permute-start(bf16[2,16,1,128]{3,1,0,2:T(8,128)(2,1)S(1)} %get-tuple-element.265), channel_id=1, source_target_pairs={{0,504},{8,0},{16,8},{24,16},{32,24},{40,32},{48,40},{56,48},{64,5... | collective-permute-start | bytes 24584 | tf_op jit(solution)/shard_map/while/body/eval_jaxpr/ppermute | solution.py:21
  466.1 12.9 %collective-permute-start = (bf16[2,16,1,128]{3,1,0,2:T(8,128)(2,1)S(1)}, bf16[2,16,1,128]{3,1,0,2:T(8,128)(2,1)S(1)}, u32[]{:S(2)}, u32[]{:S(2)}) collective-permute-start(bf16[2,16,1,128]{3,1,0,2:T(8,128)(2,1)S(1)} %get-tuple-element.265), channel_id=1, source_target_pairs={{0,504},{8,0},{16,8},{24,16},{32,24},{40,32},{48,40},{56,48},{64,5... | collective-permute-start | bytes 24584 | tf_op jit(solution)/shard_map/while/body/eval_jaxpr/ppermute | solution.py:21
  494.7 12.9 %collective-permute-start = (bf16[2,16,1,128]{3,1,0,2:T(8,128)(2,1)S(1)}, bf16[2,16,1,128]{3,1,0,2:T(8,128)(2,1)S(1)}, u32[]{:S(2)}, u32[]{:S(2)}) collective-permute-start(bf16[2,16,1,128]{3,1,0,2:T(8,128)(2,1)S(1)} %get-tuple-element.265), channel_id=1, source_target_pairs={{0,504},{8,0},{16,8},{24,16},{32,24},{40,32},{48,40},{56,48},{64,5... | collective-permute-start | bytes 24584 | tf_op jit(solution)/shard_map/while/body/eval_jaxpr/ppermute | solution.py:21
  509.0 12.9 %collective-permute-start = (bf16[2,16,1,128]{3,1,0,2:T(8,128)(2,1)S(1)}, bf16[2,16,1,128]{3,1,0,2:T(8,128)(2,1)S(1)}, u32[]{:S(2)}, u32[]{:S(2)}) collective-permute-start(bf16[2,16,1,128]{3,1,0,2:T(8,128)(2,1)S(1)} %get-tuple-element.265), channel_id=1, source_target_pairs={{0,504},{8,0},{16,8},{24,16},{32,24},{40,32},{48,40},{56,48},{64,5... | collective-permute-start | bytes 24584 | tf_op jit(solution)/shard_map/while/body/eval_jaxpr/ppermute | solution.py:21
  537.6 12.9 %collective-permute-start = (bf16[2,16,1,128]{3,1,0,2:T(8,128)(2,1)S(1)}, bf16[2,16,1,128]{3,1,0,2:T(8,128)(2,1)S(1)}, u32[]{:S(2)}, u32[]{:S(2)}) collective-permute-start(bf16[2,16,1,128]{3,1,0,2:T(8,128)(2,1)S(1)} %get-tuple-element.265), channel_id=1, source_target_pairs={{0,504},{8,0},{16,8},{24,16},{32,24},{40,32},{48,40},{56,48},{64,5... | collective-permute-start | bytes 24584 | tf_op jit(solution)/shard_map/while/body/eval_jaxpr/ppermute | solution.py:21
  551.9 12.9 %collective-permute-start = (bf16[2,16,1,128]{3,1,0,2:T(8,128)(2,1)S(1)}, bf16[2,16,1,128]{3,1,0,2:T(8,128)(2,1)S(1)}, u32[]{:S(2)}, u32[]{:S(2)}) collective-permute-start(bf16[2,16,1,128]{3,1,0,2:T(8,128)(2,1)S(1)} %get-tuple-element.265), channel_id=1, source_target_pairs={{0,504},{8,0},{16,8},{24,16},{32,24},{40,32},{48,40},{56,48},{64,5... | collective-permute-start | bytes 24584 | tf_op jit(solution)/shard_map/while/body/eval_jaxpr/ppermute | solution.py:21
  580.5 12.9 %collective-permute-start = (bf16[2,16,1,128]{3,1,0,2:T(8,128)(2,1)S(1)}, bf16[2,16,1,128]{3,1,0,2:T(8,128)(2,1)S(1)}, u32[]{:S(2)}, u32[]{:S(2)}) collective-permute-start(bf16[2,16,1,128]{3,1,0,2:T(8,128)(2,1)S(1)} %get-tuple-element.265), channel_id=1, source_target_pairs={{0,504},{8,0},{16,8},{24,16},{32,24},{40,32},{48,40},{56,48},{64,5... | collective-permute-start | bytes 24584 | tf_op jit(solution)/shard_map/while/body/eval_jaxpr/ppermute | solution.py:21
  596.2 170.4 %reduce-scatter.2.cloned.1.call-done = f32[16,33,128]{2,0,1:T(8,128)} async-done(((f32[16,33,1024]{2,0,1:T(8,128)}), f32[16,33,128]{2,0,1:T(8,128)}) %reduce-scatter.2.cloned.1.call-update) | async-done | bytes 270352 | tf_op jit(solution)/shard_map/reduce_scatter | solution.py:161
  (361 shorter events, 186.1 us)
Async XLA Ops:
  6.5 760.1 %reduce-scatter.2.cloned.1.call-start = ((), (), s32[]{:S(2)}) async-start(), calls=%async_computation.1 | async-start | bytes 2433024 | tf_op jit(solution)/shard_map/reduce_scatter | solution.py:161
  180.0 13.7 %collective-permute-start = (bf16[2,16,1,128]{3,1,0,2:T(8,128)(2,1)S(1)}, bf16[2,16,1,128]{3,1,0,2:T(8,128)(2,1)S(1)}, u32[]{:S(2)}, u32[]{:S(2)}) collective-permute-start(bf16[2,16,1,128]{3,1,0,2:T(8,128)(2,1)S(1)} %get-tuple-element.265), channel_id=1, source_target_pairs={{0,504},{8,0},{16,8},{24,16},{32,24},{40,32},{48,40},{56,48},{64,5... | collective-permute-start | bytes 24584 | tf_op jit(solution)/shard_map/while/body/eval_jaxpr/ppermute | solution.py:21
  194.3 13.7 %collective-permute-start = (bf16[2,16,1,128]{3,1,0,2:T(8,128)(2,1)S(1)}, bf16[2,16,1,128]{3,1,0,2:T(8,128)(2,1)S(1)}, u32[]{:S(2)}, u32[]{:S(2)}) collective-permute-start(bf16[2,16,1,128]{3,1,0,2:T(8,128)(2,1)S(1)} %get-tuple-element.265), channel_id=1, source_target_pairs={{0,504},{8,0},{16,8},{24,16},{32,24},{40,32},{48,40},{56,48},{64,5... | collective-permute-start | bytes 24584 | tf_op jit(solution)/shard_map/while/body/eval_jaxpr/ppermute | solution.py:21
  208.6 13.7 %collective-permute-start = (bf16[2,16,1,128]{3,1,0,2:T(8,128)(2,1)S(1)}, bf16[2,16,1,128]{3,1,0,2:T(8,128)(2,1)S(1)}, u32[]{:S(2)}, u32[]{:S(2)}) collective-permute-start(bf16[2,16,1,128]{3,1,0,2:T(8,128)(2,1)S(1)} %get-tuple-element.265), channel_id=1, source_target_pairs={{0,504},{8,0},{16,8},{24,16},{32,24},{40,32},{48,40},{56,48},{64,5... | collective-permute-start | bytes 24584 | tf_op jit(solution)/shard_map/while/body/eval_jaxpr/ppermute | solution.py:21
  222.9 13.7 %collective-permute-start = (bf16[2,16,1,128]{3,1,0,2:T(8,128)(2,1)S(1)}, bf16[2,16,1,128]{3,1,0,2:T(8,128)(2,1)S(1)}, u32[]{:S(2)}, u32[]{:S(2)}) collective-permute-start(bf16[2,16,1,128]{3,1,0,2:T(8,128)(2,1)S(1)} %get-tuple-element.265), channel_id=1, source_target_pairs={{0,504},{8,0},{16,8},{24,16},{32,24},{40,32},{48,40},{56,48},{64,5... | collective-permute-start | bytes 24584 | tf_op jit(solution)/shard_map/while/body/eval_jaxpr/ppermute | solution.py:21
  237.2 13.7 %collective-permute-start = (bf16[2,16,1,128]{3,1,0,2:T(8,128)(2,1)S(1)}, bf16[2,16,1,128]{3,1,0,2:T(8,128)(2,1)S(1)}, u32[]{:S(2)}, u32[]{:S(2)}) collective-permute-start(bf16[2,16,1,128]{3,1,0,2:T(8,128)(2,1)S(1)} %get-tuple-element.265), channel_id=1, source_target_pairs={{0,504},{8,0},{16,8},{24,16},{32,24},{40,32},{48,40},{56,48},{64,5... | collective-permute-start | bytes 24584 | tf_op jit(solution)/shard_map/while/body/eval_jaxpr/ppermute | solution.py:21
  251.5 13.7 %collective-permute-start = (bf16[2,16,1,128]{3,1,0,2:T(8,128)(2,1)S(1)}, bf16[2,16,1,128]{3,1,0,2:T(8,128)(2,1)S(1)}, u32[]{:S(2)}, u32[]{:S(2)}) collective-permute-start(bf16[2,16,1,128]{3,1,0,2:T(8,128)(2,1)S(1)} %get-tuple-element.265), channel_id=1, source_target_pairs={{0,504},{8,0},{16,8},{24,16},{32,24},{40,32},{48,40},{56,48},{64,5... | collective-permute-start | bytes 24584 | tf_op jit(solution)/shard_map/while/body/eval_jaxpr/ppermute | solution.py:21
  265.8 13.7 %collective-permute-start = (bf16[2,16,1,128]{3,1,0,2:T(8,128)(2,1)S(1)}, bf16[2,16,1,128]{3,1,0,2:T(8,128)(2,1)S(1)}, u32[]{:S(2)}, u32[]{:S(2)}) collective-permute-start(bf16[2,16,1,128]{3,1,0,2:T(8,128)(2,1)S(1)} %get-tuple-element.265), channel_id=1, source_target_pairs={{0,504},{8,0},{16,8},{24,16},{32,24},{40,32},{48,40},{56,48},{64,5... | collective-permute-start | bytes 24584 | tf_op jit(solution)/shard_map/while/body/eval_jaxpr/ppermute | solution.py:21
  280.1 13.7 %collective-permute-start = (bf16[2,16,1,128]{3,1,0,2:T(8,128)(2,1)S(1)}, bf16[2,16,1,128]{3,1,0,2:T(8,128)(2,1)S(1)}, u32[]{:S(2)}, u32[]{:S(2)}) collective-permute-start(bf16[2,16,1,128]{3,1,0,2:T(8,128)(2,1)S(1)} %get-tuple-element.265), channel_id=1, source_target_pairs={{0,504},{8,0},{16,8},{24,16},{32,24},{40,32},{48,40},{56,48},{64,5... | collective-permute-start | bytes 24584 | tf_op jit(solution)/shard_map/while/body/eval_jaxpr/ppermute | solution.py:21
  294.4 13.7 %collective-permute-start = (bf16[2,16,1,128]{3,1,0,2:T(8,128)(2,1)S(1)}, bf16[2,16,1,128]{3,1,0,2:T(8,128)(2,1)S(1)}, u32[]{:S(2)}, u32[]{:S(2)}) collective-permute-start(bf16[2,16,1,128]{3,1,0,2:T(8,128)(2,1)S(1)} %get-tuple-element.265), channel_id=1, source_target_pairs={{0,504},{8,0},{16,8},{24,16},{32,24},{40,32},{48,40},{56,48},{64,5... | collective-permute-start | bytes 24584 | tf_op jit(solution)/shard_map/while/body/eval_jaxpr/ppermute | solution.py:21
  323.1 13.7 %collective-permute-start = (bf16[2,16,1,128]{3,1,0,2:T(8,128)(2,1)S(1)}, bf16[2,16,1,128]{3,1,0,2:T(8,128)(2,1)S(1)}, u32[]{:S(2)}, u32[]{:S(2)}) collective-permute-start(bf16[2,16,1,128]{3,1,0,2:T(8,128)(2,1)S(1)} %get-tuple-element.265), channel_id=1, source_target_pairs={{0,504},{8,0},{16,8},{24,16},{32,24},{40,32},{48,40},{56,48},{64,5... | collective-permute-start | bytes 24584 | tf_op jit(solution)/shard_map/while/body/eval_jaxpr/ppermute | solution.py:21
  337.4 13.7 %collective-permute-start = (bf16[2,16,1,128]{3,1,0,2:T(8,128)(2,1)S(1)}, bf16[2,16,1,128]{3,1,0,2:T(8,128)(2,1)S(1)}, u32[]{:S(2)}, u32[]{:S(2)}) collective-permute-start(bf16[2,16,1,128]{3,1,0,2:T(8,128)(2,1)S(1)} %get-tuple-element.265), channel_id=1, source_target_pairs={{0,504},{8,0},{16,8},{24,16},{32,24},{40,32},{48,40},{56,48},{64,5... | collective-permute-start | bytes 24584 | tf_op jit(solution)/shard_map/while/body/eval_jaxpr/ppermute | solution.py:21
  366.0 13.7 %collective-permute-start = (bf16[2,16,1,128]{3,1,0,2:T(8,128)(2,1)S(1)}, bf16[2,16,1,128]{3,1,0,2:T(8,128)(2,1)S(1)}, u32[]{:S(2)}, u32[]{:S(2)}) collective-permute-start(bf16[2,16,1,128]{3,1,0,2:T(8,128)(2,1)S(1)} %get-tuple-element.265), channel_id=1, source_target_pairs={{0,504},{8,0},{16,8},{24,16},{32,24},{40,32},{48,40},{56,48},{64,5... | collective-permute-start | bytes 24584 | tf_op jit(solution)/shard_map/while/body/eval_jaxpr/ppermute | solution.py:21
  380.3 13.7 %collective-permute-start = (bf16[2,16,1,128]{3,1,0,2:T(8,128)(2,1)S(1)}, bf16[2,16,1,128]{3,1,0,2:T(8,128)(2,1)S(1)}, u32[]{:S(2)}, u32[]{:S(2)}) collective-permute-start(bf16[2,16,1,128]{3,1,0,2:T(8,128)(2,1)S(1)} %get-tuple-element.265), channel_id=1, source_target_pairs={{0,504},{8,0},{16,8},{24,16},{32,24},{40,32},{48,40},{56,48},{64,5... | collective-permute-start | bytes 24584 | tf_op jit(solution)/shard_map/while/body/eval_jaxpr/ppermute | solution.py:21
  394.6 13.7 %collective-permute-start = (bf16[2,16,1,128]{3,1,0,2:T(8,128)(2,1)S(1)}, bf16[2,16,1,128]{3,1,0,2:T(8,128)(2,1)S(1)}, u32[]{:S(2)}, u32[]{:S(2)}) collective-permute-start(bf16[2,16,1,128]{3,1,0,2:T(8,128)(2,1)S(1)} %get-tuple-element.265), channel_id=1, source_target_pairs={{0,504},{8,0},{16,8},{24,16},{32,24},{40,32},{48,40},{56,48},{64,5... | collective-permute-start | bytes 24584 | tf_op jit(solution)/shard_map/while/body/eval_jaxpr/ppermute | solution.py:21
  408.9 13.7 %collective-permute-start = (bf16[2,16,1,128]{3,1,0,2:T(8,128)(2,1)S(1)}, bf16[2,16,1,128]{3,1,0,2:T(8,128)(2,1)S(1)}, u32[]{:S(2)}, u32[]{:S(2)}) collective-permute-start(bf16[2,16,1,128]{3,1,0,2:T(8,128)(2,1)S(1)} %get-tuple-element.265), channel_id=1, source_target_pairs={{0,504},{8,0},{16,8},{24,16},{32,24},{40,32},{48,40},{56,48},{64,5... | collective-permute-start | bytes 24584 | tf_op jit(solution)/shard_map/while/body/eval_jaxpr/ppermute | solution.py:21
  423.2 13.7 %collective-permute-start = (bf16[2,16,1,128]{3,1,0,2:T(8,128)(2,1)S(1)}, bf16[2,16,1,128]{3,1,0,2:T(8,128)(2,1)S(1)}, u32[]{:S(2)}, u32[]{:S(2)}) collective-permute-start(bf16[2,16,1,128]{3,1,0,2:T(8,128)(2,1)S(1)} %get-tuple-element.265), channel_id=1, source_target_pairs={{0,504},{8,0},{16,8},{24,16},{32,24},{40,32},{48,40},{56,48},{64,5... | collective-permute-start | bytes 24584 | tf_op jit(solution)/shard_map/while/body/eval_jaxpr/ppermute | solution.py:21
  451.8 13.7 %collective-permute-start = (bf16[2,16,1,128]{3,1,0,2:T(8,128)(2,1)S(1)}, bf16[2,16,1,128]{3,1,0,2:T(8,128)(2,1)S(1)}, u32[]{:S(2)}, u32[]{:S(2)}) collective-permute-start(bf16[2,16,1,128]{3,1,0,2:T(8,128)(2,1)S(1)} %get-tuple-element.265), channel_id=1, source_target_pairs={{0,504},{8,0},{16,8},{24,16},{32,24},{40,32},{48,40},{56,48},{64,5... | collective-permute-start | bytes 24584 | tf_op jit(solution)/shard_map/while/body/eval_jaxpr/ppermute | solution.py:21
  466.1 13.7 %collective-permute-start = (bf16[2,16,1,128]{3,1,0,2:T(8,128)(2,1)S(1)}, bf16[2,16,1,128]{3,1,0,2:T(8,128)(2,1)S(1)}, u32[]{:S(2)}, u32[]{:S(2)}) collective-permute-start(bf16[2,16,1,128]{3,1,0,2:T(8,128)(2,1)S(1)} %get-tuple-element.265), channel_id=1, source_target_pairs={{0,504},{8,0},{16,8},{24,16},{32,24},{40,32},{48,40},{56,48},{64,5... | collective-permute-start | bytes 24584 | tf_op jit(solution)/shard_map/while/body/eval_jaxpr/ppermute | solution.py:21
  494.7 13.7 %collective-permute-start = (bf16[2,16,1,128]{3,1,0,2:T(8,128)(2,1)S(1)}, bf16[2,16,1,128]{3,1,0,2:T(8,128)(2,1)S(1)}, u32[]{:S(2)}, u32[]{:S(2)}) collective-permute-start(bf16[2,16,1,128]{3,1,0,2:T(8,128)(2,1)S(1)} %get-tuple-element.265), channel_id=1, source_target_pairs={{0,504},{8,0},{16,8},{24,16},{32,24},{40,32},{48,40},{56,48},{64,5... | collective-permute-start | bytes 24584 | tf_op jit(solution)/shard_map/while/body/eval_jaxpr/ppermute | solution.py:21
  509.0 13.7 %collective-permute-start = (bf16[2,16,1,128]{3,1,0,2:T(8,128)(2,1)S(1)}, bf16[2,16,1,128]{3,1,0,2:T(8,128)(2,1)S(1)}, u32[]{:S(2)}, u32[]{:S(2)}) collective-permute-start(bf16[2,16,1,128]{3,1,0,2:T(8,128)(2,1)S(1)} %get-tuple-element.265), channel_id=1, source_target_pairs={{0,504},{8,0},{16,8},{24,16},{32,24},{40,32},{48,40},{56,48},{64,5... | collective-permute-start | bytes 24584 | tf_op jit(solution)/shard_map/while/body/eval_jaxpr/ppermute | solution.py:21
  537.6 13.7 %collective-permute-start = (bf16[2,16,1,128]{3,1,0,2:T(8,128)(2,1)S(1)}, bf16[2,16,1,128]{3,1,0,2:T(8,128)(2,1)S(1)}, u32[]{:S(2)}, u32[]{:S(2)}) collective-permute-start(bf16[2,16,1,128]{3,1,0,2:T(8,128)(2,1)S(1)} %get-tuple-element.265), channel_id=1, source_target_pairs={{0,504},{8,0},{16,8},{24,16},{32,24},{40,32},{48,40},{56,48},{64,5... | collective-permute-start | bytes 24584 | tf_op jit(solution)/shard_map/while/body/eval_jaxpr/ppermute | solution.py:21
  551.9 13.7 %collective-permute-start = (bf16[2,16,1,128]{3,1,0,2:T(8,128)(2,1)S(1)}, bf16[2,16,1,128]{3,1,0,2:T(8,128)(2,1)S(1)}, u32[]{:S(2)}, u32[]{:S(2)}) collective-permute-start(bf16[2,16,1,128]{3,1,0,2:T(8,128)(2,1)S(1)} %get-tuple-element.265), channel_id=1, source_target_pairs={{0,504},{8,0},{16,8},{24,16},{32,24},{40,32},{48,40},{56,48},{64,5... | collective-permute-start | bytes 24584 | tf_op jit(solution)/shard_map/while/body/eval_jaxpr/ppermute | solution.py:21
  580.5 13.7 %collective-permute-start = (bf16[2,16,1,128]{3,1,0,2:T(8,128)(2,1)S(1)}, bf16[2,16,1,128]{3,1,0,2:T(8,128)(2,1)S(1)}, u32[]{:S(2)}, u32[]{:S(2)}) collective-permute-start(bf16[2,16,1,128]{3,1,0,2:T(8,128)(2,1)S(1)} %get-tuple-element.265), channel_id=1, source_target_pairs={{0,504},{8,0},{16,8},{24,16},{32,24},{40,32},{48,40},{56,48},{64,5... | collective-permute-start | bytes 24584 | tf_op jit(solution)/shard_map/while/body/eval_jaxpr/ppermute | solution.py:21
  (14 other events, 258.5 us)
Sparse Core Ops, SparseCore 0:
  596.3 170.2 reduce-scatter.1
where the time goes:
time: 775 us; the launch traced here: 773 us
  starting transfers between devices  392 us (51%)
  waiting for transfers between devices  200 us (26%)
  blocking collectives  129 us (17%)
  matrix products  19.9 us (3%)
  between operations  15.7 us (2%)
  local copies, waits for them, and re-layouts  11.2 us (1%)
    ppermute x32, starting transfers between devices, from_behind(): lax.ppermute(shard, axis, [(i, (i + by) % count) for i in range(count)])  386 us
    reduce_scatter x1, waiting for transfers between devices, body(): results = lax.psum_scatter(results, 'seg', scatter_dimension=2, tiled=True)  170 us
    all_gather x1, blocking collectives, body(): all_strips = lax.all_gather(strips[None], 'chan', axis=0, tiled=True)  129 us
    ppermute x32, waiting for transfers between devices, from_behind(): lax.ppermute(shard, axis, [(i, (i + by) % count) for i in range(count)])  29.5 us
  transfers between devices with their start and end apart: 35, of which 33 were waited for; matrix products, arithmetic and copies ran while one was open for 0% of the time, Pallas kernels for 0%

commit v1 on v0

v1 whole, which is shorter than its diff:
```python
import functools
import math

import jax
import jax.numpy as jnp
import numpy as np
from jax import lax
from jax.experimental import pallas as pl
from jax.experimental.pallas import tpu as pltpu
from jax.sharding import PartitionSpec as P

WIN = 256
NLAG = 64
FILT = 64
BAND = 4
F = 128
C = 16
TPAD = 264
MESH = pl.DeviceIdType.MESH
F32 = jnp.float32
BF16 = jnp.bfloat16


def split_bf16(table):
    hi = np.asarray(table, np.float32).astype(BF16)
    lo = (np.asarray(table, np.float32) - hi.astype(np.float32)).astype(BF16)
    return hi, lo


def dft_table():
    phases = np.arange(WIN)[:, None] * np.arange(F)[None, :] % WIN
    angles = phases * (2.0 * math.pi / WIN)
    return np.concatenate([np.cos(angles), -np.sin(angles)], axis=1)


def lag_table(partners, scale):
    phases = (np.arange(F)[:, None] * (np.arange(NLAG)[None, :] - NLAG // 2)) % WIN
    angles = phases * (2.0 * math.pi / WIN)
    gains = np.where(np.arange(F) == 0, 1.0, 2.0)[:, None] * scale
    one = np.concatenate([gains * np.cos(angles), -gains * np.sin(angles)], axis=0)
    return np.kron(np.eye(partners), one)


def dot(a, b):
    return jnp.dot(a, b, preferred_element_type=F32)


def build_weights(w_first, w_mid, w_last, w1f, w1, wm, w3):
    first = w_first[...].astype(F32)
    w1f[...] = jnp.zeros(w1f.shape, F32)
    for qq in range(3):
        taps = jnp.concatenate([first[3 * p + qq : 3 * p + qq + 1] for p in range(3)], axis=0)
        for late in range(3):
            for row in range(20):
                at = (late + qq) * 24 + row
                w1f[at : at + 3, late * 1280 + row * 64 : late * 1280 + row * 64 + 64] = taps
    w1[...] = w1f[...].astype(BF16)
    wm[...] = jnp.zeros(wm.shape, BF16)
    for q in range(3):
        for j in range(4):
            for p in range(3):
                wm[q, (j + p) * 64 : (j + p + 1) * 64, j * 64 : (j + 1) * 64] = w_mid[0, 3 * p + q]
    last = jnp.concatenate([w_last[...].astype(F32), jnp.zeros((9, 64), F32)], axis=1)
    last = jnp.concatenate([last, jnp.zeros((7, 128), F32)], axis=0)
    taps_t = jnp.transpose(last)[:64]
    lane = lax.broadcasted_iota(jnp.int32, (64, 128), 1)
    for q in range(3):
        base = jnp.zeros((64, 128), F32)
        for p in range(3):
            col = jnp.broadcast_to(taps_t[:, 3 * p + q : 3 * p + q + 1], (64, 128))
            base = jnp.where(lane == 2 - p, col, base)
        for row in range(18):
            rolled = pltpu.roll(base, (row - 2) % 128, axis=1)
            w3[row * 64 : (row + 1) * 64, q * 128 : (q + 1) * 128] = rolled.astype(BF16)


def convolve(ext, shifted, w1, wm, w3, h1, h2, acc):
    whole = ext[...]
    for q in range(5):
        shifted[q * 24 : (q + 1) * 24, :] = pltpu.roll(whole, (3 - q) % 384, axis=1)
    shifted[120:128, :] = jnp.zeros((8, 384), F32)
    patches = jnp.transpose(shifted[...])[:TPAD].astype(BF16)
    for block in range(15):
        cols = slice(block * 256, (block + 1) * 256)
        h1[:, cols] = jnp.maximum(dot(patches, w1[:, cols]), 0.0).astype(BF16)
    for group in range(5):
        depth, width = (384, 256) if group < 4 else (256, 128)
        total = None
        for q in range(3):
            at = q * 1280 + group * 256
            part = dot(h1[:, at : at + depth], wm[q, :depth, :width])
            total = part if total is None else total + part
        h2[:, group * 256 : group * 256 + width] = jnp.maximum(total, 0.0).astype(BF16)
    acc[...] = dot(h2[...], w3[...])
    noise_t = acc[0:256, 0:128] + acc[1:257, 128:256] + acc[2:258, 256:384]
    return jnp.transpose(noise_t)[:C]


def whiten(detrended, table_hi, table_lo):
    hi = detrended.astype(BF16)
    lo = (detrended - hi.astype(F32)).astype(BF16)
    spec = dot(hi, table_hi[...]) + (dot(lo, table_hi[...]) + dot(hi, table_lo[...]))
    re, im = spec[:, :F], spec[:, F:]
    power = re * re + im * im
    lane = lax.broadcasted_iota(jnp.int32, (C, F), 1)
    smooth = power
    for by in range(1, BAND + 1):
        smooth = smooth + jnp.where(lane >= by, pltpu.roll(power, by, axis=1), 0.0)
        smooth = smooth + jnp.where(lane < F - by, pltpu.roll(power, F - by, axis=1), 0.0)
    mean = jnp.sum(power, axis=1, keepdims=True) * (1.0 / F)
    divisor = jnp.sqrt(smooth * (1.0 / (2 * BAND + 1)) + 0.1 * mean + 1e-6)
    return jnp.concatenate([re / divisor, im / divisor], axis=1).astype(BF16)


def kernel(
    dims, raw, w_first, w_mid, w_last, lower, upper, valid, dft_hi, dft_lo, lag_hi, lag_lo, out,
    masked, packet, zbuf, xsend, xbuf, strip, own_l, own_r, strip_l, strip_r,
    w1f, w1, wm, w3, ext, shifted, h1, h2, acc, spec, xall, xf, mine, got, gf, lhs,
    z_send, z_recv, x_send, x_recv, h_send, h_recv, s_send, s_recv, c_send, c_recv,
):
    n_chan, n_seg, n_x = dims
    n_r = n_chan // n_x
    half = n_chan // 2
    partners = C // n_seg
    chan, seg = lax.axis_index("chan"), lax.axis_index("seg")
    slab = lax.div(chan, n_r)
    place = lax.rem(chan, n_r)

    def z_peer(k):
        return slab * n_r + lax.rem(place + k, n_r)

    def x_peer(k):
        return lax.rem(slab + k, n_x) * n_r + place

    def seg_peer(k):
        return lax.rem(seg + k, n_seg)

    barrier = pltpu.get_barrier_semaphore()

    def greet(peer_of, count, along):
        def one(k, carry):
            to = (peer_of(k), seg) if along == "chan" else (chan, peer_of(k))
            pl.semaphore_signal(barrier, inc=1, device_id=to, device_id_type=MESH)
            return carry
        lax.fori_loop(1, count, one, 0)

    greet(z_peer, n_r, "chan")
    greet(x_peer, n_x, "chan")
    greet(seg_peer, n_seg, "seg")

    live = (lax.broadcasted_iota(jnp.int32, (C, WIN), 0) < valid[0]).astype(F32)
    own = raw[...].astype(F32) * live
    masked[...] = own.astype(BF16)
    row8 = lax.broadcasted_iota(jnp.int32, (8, WIN), 0)
    outer = jnp.concatenate([own[13:16], own[0:3], own[0:2]], axis=0)
    outer = jnp.where(row8 == 6, upper[0].astype(F32), outer)
    outer = jnp.where(row8 == 7, lower[0].astype(F32), outer)
    packet[...] = outer.astype(BF16)
    zbuf[place] = outer.astype(BF16)

    pl.semaphore_wait(barrier, n_r + n_x + n_seg - 3)

    def z_copy(k):
        return pltpu.make_async_remote_copy(
            packet, zbuf.at[place], z_send.at[k], z_recv.at[k],
            device_id=(z_peer(k), seg), device_id_type=MESH,
        )

    def x_copy(k):
        return pltpu.make_async_remote_copy(
            xsend.at[k], xbuf.at[k], x_send.at[k], x_recv.at[k],
            device_id=(x_peer(k), seg), device_id_type=MESH,
        )

    def halo_copy(which):
        source, target, step = [
            (masked.at[:, 0:128], own_r, n_seg - 1),
            (masked.at[:, 128:256], own_l, 1),
            (strip.at[:, 0:128], strip_r, n_seg - 1),
            (strip.at[:, 128:256], strip_l, 1),
        ][which]
        return pltpu.make_async_remote_copy(
            source, target, h_send.at[which], h_recv.at[which],
            device_id=(chan, seg_peer(step)), device_id_type=MESH,
        )

    def each(first, last, act):
        def one(k, carry):
            act(k)
            return carry
        lax.fori_loop(first, last, one, 0)

    each(1, n_r, lambda k: z_copy(k).start())
    halo_copy(0).start()
    halo_copy(1).start()

    build_weights(w_first, w_mid, w_last, w1f, w1, wm, w3)

    each(1, n_r, lambda k: z_copy(k).wait_recv())
    wanted = [x_peer(k).astype(F32) for k in range(n_x)]
    picked = [jnp.zeros((8, WIN), F32) for _ in range(n_x)]
    for source in range(n_r):
        values = zbuf[source].astype(F32)
        goes = jnp.where(
            row8 < 3,
            jnp.broadcast_to(values[6:7], (8, WIN)),
            jnp.broadcast_to(values[7:8], (8, WIN)),
        )
        picked = [p + jnp.where(goes == w, values, 0.0) for p, w in zip(picked, wanted)]
    for k in range(1, n_x):
        xsend[k] = picked[k].astype(BF16)
        x_copy(k).start()
    strips = picked[0]
    for k in range(1, n_x):
        x_copy(k).wait_recv()
        strips = strips + xbuf[k].astype(F32)
    strip[...] = strips.astype(BF16)
    halo_copy(2).start()
    halo_copy(3).start()

    def edges(before, after, rows):
        lane = lax.broadcasted_iota(jnp.int32, (rows, 128), 1)
        has_before = (seg > 0).astype(F32)
        has_after = (seg < n_seg - 1).astype(F32)
        late = jnp.where(lane < 3, after[...].astype(F32) * has_after, 0.0)
        return jnp.where(lane >= 125, before[...].astype(F32) * has_before, late)

    halo_copy(0).wait_recv()
    halo_copy(1).wait_recv()
    ext[3:19, 0:256] = own
    ext[3:19, 256:384] = edges(own_l, own_r, C)
    ext[22:24, :] = jnp.zeros((2, 384), F32)
    halo_copy(2).wait_recv()
    halo_copy(3).wait_recv()
    strip_edge = edges(strip_l, strip_r, 8)
    ext[0:3, 0:256] = strips[0:3]
    ext[0:3, 256:384] = strip_edge[0:3]
    ext[19:22, 0:256] = strips[3:6]
    ext[19:22, 256:384] = strip_edge[3:6]

    noise = convolve(ext, shifted, w1, wm, w3, h1, h2, acc)
    clean = (own - noise) * live
    common = jnp.sum(clean, axis=0, keepdims=True) / valid[0].astype(F32)
    detrended = (clean - common) * live
    spectra = whiten(detrended, dft_hi, dft_lo)
    spec[...] = spectra
    xall[seg] = spectra

    def s_copy(k):
        return pltpu.make_async_remote_copy(
            spec, xall.at[seg], s_send.at[k], s_recv.at[k],
            device_id=(chan, seg_peer(k)), device_id_type=MESH,
        )

    each(1, n_seg, lambda k: s_copy(k).start())
    each(1, n_seg, lambda k: s_copy(k).wait_recv())

    flat = xall[...].reshape(n_seg * C, 2 * F)
    r_id = lax.broadcasted_iota(jnp.int32, (C, n_seg * C), 0)
    c_id = lax.broadcasted_iota(jnp.int32, (C, n_seg * C), 1)
    source_row = (r_id // partners) * C + seg * partners + r_id % partners
    chosen = dot((c_id == source_row).astype(F32).astype(BF16), flat).astype(BF16)
    mine[...] = chosen
    got[0] = chosen

    def c_copy(d):
        return pltpu.make_async_remote_copy(
            mine, got.at[d], c_send.at[d], c_recv.at[d],
            device_id=(lax.rem(chan + n_chan - d, n_chan), seg), device_id_type=MESH,
        )

    each(1, half + 1, lambda d: c_copy(d).start())
    xf[...] = xall[...].astype(F32)

    def correlate(d):
        gf[...] = got[d].astype(F32)
        at = pl.multiple_of(d * C, C)
        for b in range(partners):
            cr = jnp.zeros((C, F), F32)
            ci = jnp.zeros((C, F), F32)
            for w in range(n_seg):
                row = w * partners + b
                pr = jnp.broadcast_to(gf[row : row + 1, 0:F], (C, F))
                pi = jnp.broadcast_to(gf[row : row + 1, F : 2 * F], (C, F))
                ar, ai = xf[w, :, 0:F], xf[w, :, F : 2 * F]
                cr = cr + (ar * pr + ai * pi)
                ci = ci + (ai * pr - ar * pi)
            lhs[pl.ds(at, C), b * 256 : b * 256 + F] = cr
            lhs[pl.ds(at, C), b * 256 + F : b * 256 + 2 * F] = ci

    correlate(0)

    def arrived(d):
        c_copy(d).wait_recv()
        correlate(d)

    each(1, half + 1, arrived)

    chunk = next(c for c in range(11, 0, -1) if (half + 1) % c == 0)
    for start in range(0, half + 1, chunk):
        values = lhs[start * C : (start + chunk) * C, :]
        hi = values.astype(BF16)
        lo = (values - hi.astype(F32)).astype(BF16)
        lagged = dot(hi, lag_hi[...]) + (dot(lo, lag_hi[...]) + dot(hi, lag_lo[...]))
        for d in range(chunk):
            out[:, start + d, :] = lagged[d * C : (d + 1) * C]

    each(1, n_r, lambda k: z_copy(k).wait_send())
    for k in range(1, n_x):
        x_copy(k).wait_send()
    for which in range(4):
        halo_copy(which).wait_send()
    each(1, n_seg, lambda k: s_copy(k).wait_send())
    each(1, half + 1, lambda d: c_copy(d).wait_send())


def body(raw, w_first, w_mid, w_last, lower, upper, valid, dims):
    n_chan, n_seg, n_x = dims
    n_r = n_chan // n_x
    half = n_chan // 2
    partners = C // n_seg
    dft_hi, dft_lo = split_bf16(dft_table())
    lag_hi, lag_lo = split_bf16(lag_table(partners, 1.0 / math.sqrt(n_seg * F)))
    vmem = pl.BlockSpec(memory_space=pltpu.VMEM)
    smem = pl.BlockSpec(memory_space=pltpu.SMEM)
    dma = pltpu.SemaphoreType.DMA
    scratch = [
        pltpu.VMEM((C, WIN), BF16),
        pltpu.VMEM((8, WIN), BF16),
        pltpu.VMEM((n_r, 8, WIN), BF16),
        pltpu.VMEM((n_x, 8, WIN), BF16),
        pltpu.VMEM((n_x, 8, WIN), BF16),
        pltpu.VMEM((8, WIN), BF16),
        pltpu.VMEM((C, 128), BF16),
        pltpu.VMEM((C, 128), BF16),
        pltpu.VMEM((8, 128), BF16),
        pltpu.VMEM((8, 128), BF16),
        pltpu.VMEM((128, 3840), F32),
        pltpu.VMEM((128, 3840), BF16),
        pltpu.VMEM((3, 384, 256), BF16),
        pltpu.VMEM((1152, 384), BF16),
        pltpu.VMEM((24, 384), F32),
        pltpu.VMEM((128, 384), F32),
        pltpu.VMEM((TPAD, 3840), BF16),
        pltpu.VMEM((TPAD, 1152), BF16),
        pltpu.VMEM((TPAD, 384), F32),
        pltpu.VMEM((C, 2 * F), BF16),
        pltpu.VMEM((n_seg, C, 2 * F), BF16),
        pltpu.VMEM((n_seg, C, 2 * F), F32),
        pltpu.VMEM((C, 2 * F), BF16),
        pltpu.VMEM((half + 1, C, 2 * F), BF16),
        pltpu.VMEM((C, 2 * F), F32),
        pltpu.VMEM(((half + 1) * C, partners * 2 * F), F32),
        dma((n_r,)), dma((n_r,)), dma((n_x,)), dma((n_x,)), dma((4,)), dma((4,)),
        dma((n_seg,)), dma((n_seg,)), dma((half + 1,)), dma((half + 1,)),
    ]
    return pl.pallas_call(
        functools.partial(kernel, dims),
        out_shape=jax.ShapeDtypeStruct((C, half + 1, partners * NLAG), F32),
        in_specs=[vmem] * 4 + [smem] * 3 + [vmem] * 4,
        out_specs=vmem,
        scratch_shapes=scratch,
        compiler_params=pltpu.CompilerParams(
            collective_id=0, has_side_effects=True, vmem_limit_bytes=48 << 20
        ),
    )(
        raw, w_first, w_mid, w_last, lower, upper, valid,
        jnp.asarray(dft_hi), jnp.asarray(dft_lo), jnp.asarray(lag_hi), jnp.asarray(lag_lo),
    )


def solution(mesh):
    n_chan, n_seg = mesh.shape["chan"], mesh.shape["seg"]
    dims = (n_chan, n_seg, 4 if n_chan % 4 == 0 and n_chan >= 16 else 2)
    return jax.shard_map(
        functools.partial(body, dims=dims),
        mesh=mesh,
        in_specs=(P("chan", "seg"), P(), P(), P(), P("chan"), P("chan"), P("chan")),
        out_specs=P("chan", None, "seg"),
        check_vma=False,
    )
```

time: 775 us -> 71.1 us (0.09)
  starting transfers between devices: 392 us -> 0 us
  waiting for transfers between devices: 200 us -> 0 us
  blocking collectives: 129 us -> 0 us
  Pallas kernels: 0 us -> 62.2 us
  matrix products: 19.9 us -> 0 us
  between operations: 15.7 us -> 1.99 us
    ppermute x34 -> x0, starting transfers between devices: 392 us -> none  [the longest x32 386 us: from_behind(): lax.ppermute(shard, axis, [(i, (i + by) % count) for i in range(count)])]
    reduce_scatter x1 -> x0, waiting for transfers between devices: 170 us -> none  [body(): results = lax.psum_scatter(results, 'seg', scatter_dimension=2, tiled=True)]
    all_gather x1 -> x0, blocking collectives: 129 us -> none  [body(): all_strips = lax.all_gather(strips[None], 'chan', axis=0, tiled=True)]
    pallas_call x0 -> x1, Pallas kernels: none -> 62.2 us  [body(): pl.pallas_call(functools.partial(kernel, dims), out_shape=jax.ShapeDtypeS...]
    ppermute x34 -> x0, waiting for transfers between devices: 29.5 us -> none  [the longest x32 29.5 us: from_behind(): lax.ppermute(shard, axis, [(i, (i + by) % count) for i in range(count)])]
    dot_general x45 -> x0, matrix products: 19.9 us -> none  [the longest x33 12.5 us: correlate(): jnp.dot(stacked_parts.reshape(-1, stacked_parts.shape[2]), lag_weights, p...]
  transfers between devices with their start and end apart: 35 -> 0, of which waited for: 33 -> 0; matrix products, arithmetic and copies ran while one was open for 0% -> 0% of each run, Pallas kernels for 0% -> 0%
where the time goes in v1:
time: 71.1 us; the launch traced here: 70.8 us
  Pallas kernels  62.2 us (87%)
  local copies, waits for them, and re-layouts  6.66 us (9%)
  between operations  1.99 us (3%)
    pallas_call x1, Pallas kernels, body(): pl.pallas_call(functools.partial(kernel, dims), out_shape=jax.ShapeDtypeS...  62.2 us
    unnamed x16, local copies, waits for them, and re-layouts  5.9 us

profile of v1, /device:TPU:1, one launch (start us, length us, event | category | flops | bytes accessed | tf_op | source)
XLA Modules:
  0.0 70.8 jit_solution(3553748514738500618)
XLA Ops:
  0.0 0.0 copy-start.6
  2.0 0.0 copy-done.6
  2.0 0.0 copy-start
  2.0 0.9 %copy-done = bf16[1,9,64,64]{3,2,1,0:T(8,128)(2,1)S(1)} copy-done((bf16[1,9,64,64]{3,2,1,0:T(8,128)(2,1)S(1)}, bf16[1,9,64,64]{3,2,1,0:T(8,128)(2,1)}, u32[]{:S(2)}) %copy-start) | copy-done | bytes 73752
  2.9 0.0 copy-start.1
  2.9 0.9 %copy-done.1 = bf16[512,128]{1,0:T(8,128)(2,1)S(1)} copy-done((bf16[512,128]{1,0:T(8,128)(2,1)S(1)}, bf16[512,128]{1,0:T(8,128)(2,1)}, u32[]{:S(2)}) %copy-start.1) | copy-done | bytes 131096
  3.8 0.0 copy-start.2
  3.8 0.9 %copy-done.2 = bf16[512,128]{1,0:T(8,128)(2,1)S(1)} copy-done((bf16[512,128]{1,0:T(8,128)(2,1)S(1)}, bf16[512,128]{1,0:T(8,128)(2,1)}, u32[]{:S(2)}) %copy-start.2) | copy-done | bytes 131096
  4.7 0.0 copy-start.3
  4.7 0.9 %copy-done.3 = bf16[256,256]{1,0:T(8,128)(2,1)S(1)} copy-done((bf16[256,256]{1,0:T(8,128)(2,1)S(1)}, bf16[256,256]{1,0:T(8,128)(2,1)}, u32[]{:S(2)}) %copy-start.3) | copy-done | bytes 131096
  5.6 0.0 copy-start.4
  5.6 0.9 %copy-done.4 = bf16[256,256]{1,0:T(8,128)(2,1)S(1)} copy-done((bf16[256,256]{1,0:T(8,128)(2,1)S(1)}, bf16[256,256]{1,0:T(8,128)(2,1)}, u32[]{:S(2)}) %copy-start.4) | copy-done | bytes 131096
  6.5 0.0 copy-start.5
  6.5 0.7 copy-done.5
  7.2 0.0 copy-start.7
  7.2 0.7 copy-done.7
  7.9 62.2 %shard_map.109 = f32[16,33,128]{2,1,0:T(8,128)S(1)} custom-call(bf16[16,256]{1,0:T(8,128)(2,1)S(1)} %copy-done.5, bf16[9,64]{1,0:T(8,128)(2,1)S(1)} %copy-done.6, bf16[1,9,64,64]{3,2,1,0:T(8,128)(2,1)S(1)} %copy-done, bf16[9,64]{1,0:T(8,128)(2,1)S(1)} %copy-done.7, s32[1]{0:T(128)S(6)} %copy.13.lower, s32[1]{0:T(128)S(6)} %copy.14.upper, s32[1]{0:T(128)S(6)} %copy.15.valid, ...), custom_call_target="tpu_custom_call" | custom-call | tf_op jit(solution)/shard_map/pallas_call | solution.py:357
  70.0 0.8 %copy.12 = f32[16,33,128]{2,0,1:T(8,128)} copy(f32[16,33,128]{2,1,0:T(8,128)S(1)} %shard_map.109) | data formatting | bytes 540672 | tf_op jit(solution)/shard_map/pallas_call | solution.py:357
Async XLA Ops:
  0.0 2.0 %copy-start.6 = (bf16[9,64]{1,0:T(8,128)(2,1)S(1)}, bf16[9,64]{1,0:T(8,128)(2,1)}, u32[]{:S(2)}) copy-start(bf16[9,64]{1,0:T(8,128)(2,1)} %w_first.1) | copy-start | bytes 3460
  2.0 0.9 %copy-start = (bf16[1,9,64,64]{3,2,1,0:T(8,128)(2,1)S(1)}, bf16[1,9,64,64]{3,2,1,0:T(8,128)(2,1)}, u32[]{:S(2)}) copy-start(bf16[1,9,64,64]{3,2,1,0:T(8,128)(2,1)} %w_mid.1) | copy-start | bytes 221188
  2.9 0.9 %copy-start.1 = (bf16[512,128]{1,0:T(8,128)(2,1)S(1)}, bf16[512,128]{1,0:T(8,128)(2,1)}, u32[]{:S(2)}) copy-start(bf16[512,128]{1,0:T(8,128)(2,1)} %constant.11.clone.lag_lo) | copy-start | bytes 393220
  3.8 0.9 %copy-start.2 = (bf16[512,128]{1,0:T(8,128)(2,1)S(1)}, bf16[512,128]{1,0:T(8,128)(2,1)}, u32[]{:S(2)}) copy-start(bf16[512,128]{1,0:T(8,128)(2,1)} %constant.10.clone.lag_hi) | copy-start | bytes 393220
  4.7 0.9 %copy-start.3 = (bf16[256,256]{1,0:T(8,128)(2,1)S(1)}, bf16[256,256]{1,0:T(8,128)(2,1)}, u32[]{:S(2)}) copy-start(bf16[256,256]{1,0:T(8,128)(2,1)} %constant.9.clone.dft_lo) | copy-start | bytes 393220
  5.6 0.9 %copy-start.4 = (bf16[256,256]{1,0:T(8,128)(2,1)S(1)}, bf16[256,256]{1,0:T(8,128)(2,1)}, u32[]{:S(2)}) copy-start(bf16[256,256]{1,0:T(8,128)(2,1)} %constant.8.clone.dft_hi) | copy-start | bytes 393220
  6.5 0.7 copy-start.5
  7.2 0.7 copy-start.7

commit v2 on v1

v2 whole, which is shorter than its diff:
```python
import functools
import math

import jax
import jax.numpy as jnp
import numpy as np
from jax import lax
from jax.experimental import pallas as pl
from jax.experimental.pallas import tpu as pltpu
from jax.sharding import PartitionSpec as P

WIN = 256
NLAG = 64
FILT = 64
BAND = 4
F = 128
C = 16
TPAD = 264
MESH = pl.DeviceIdType.MESH
F32 = jnp.float32
BF16 = jnp.bfloat16


def split_bf16(table):
    hi = np.asarray(table, np.float32).astype(BF16)
    lo = (np.asarray(table, np.float32) - hi.astype(np.float32)).astype(BF16)
    return np.stack([hi, lo])


def dft_table():
    phases = np.arange(WIN)[:, None] * np.arange(F)[None, :] % WIN
    angles = phases * (2.0 * math.pi / WIN)
    return np.concatenate([np.cos(angles), -np.sin(angles)], axis=1)


def lag_table(partners, scale):
    phases = (np.arange(F)[:, None] * (np.arange(NLAG)[None, :] - NLAG // 2)) % WIN
    angles = phases * (2.0 * math.pi / WIN)
    gains = np.where(np.arange(F) == 0, 1.0, 2.0)[:, None] * scale
    one = np.concatenate([gains * np.cos(angles), -gains * np.sin(angles)], axis=0)
    return np.kron(np.eye(partners), one)


def dot(a, b):
    return jnp.dot(a, b, preferred_element_type=F32)


def build_weights(w_first, w_mid, w_last, w1f, w1, wm, w3):
    first = w_first[...].astype(F32)
    w1f[...] = jnp.zeros(w1f.shape, F32)
    for qq in range(3):
        taps = jnp.concatenate([first[3 * p + qq : 3 * p + qq + 1] for p in range(3)], axis=0)
        for late in range(3):
            for row in range(20):
                at = (late + qq) * 24 + row
                w1f[at : at + 3, late * 1280 + row * 64 : late * 1280 + row * 64 + 64] = taps
    w1[...] = w1f[...].astype(BF16)
    wm[...] = jnp.zeros(wm.shape, BF16)
    for q in range(3):
        for j in range(4):
            for p in range(3):
                wm[q, (j + p) * 64 : (j + p + 1) * 64, j * 64 : (j + 1) * 64] = w_mid[0, 3 * p + q]
    last = jnp.concatenate([w_last[...].astype(F32), jnp.zeros((9, 64), F32)], axis=1)
    last = jnp.concatenate([last, jnp.zeros((7, 128), F32)], axis=0)
    taps_t = jnp.transpose(last)[:64]
    lane = lax.broadcasted_iota(jnp.int32, (64, 128), 1)
    for q in range(3):
        base = jnp.zeros((64, 128), F32)
        for p in range(3):
            col = jnp.broadcast_to(taps_t[:, 3 * p + q : 3 * p + q + 1], (64, 128))
            base = jnp.where(lane == 2 - p, col, base)
        for row in range(18):
            rolled = pltpu.roll(base, (row - 2) % 128, axis=1)
            w3[row * 64 : (row + 1) * 64, q * 128 : (q + 1) * 128] = rolled.astype(BF16)


def convolve(ext, shifted, w1, wm, w3, h1, h2, acc):
    whole = ext[...]
    for q in range(5):
        shifted[q * 24 : (q + 1) * 24, :] = pltpu.roll(whole, (3 - q) % 384, axis=1)
    shifted[120:128, :] = jnp.zeros((8, 384), F32)
    patches = jnp.transpose(shifted[...])[:TPAD].astype(BF16)
    for block in range(15):
        cols = slice(block * 256, (block + 1) * 256)
        h1[:, cols] = jnp.maximum(dot(patches, w1[:, cols]), 0.0).astype(BF16)
    for group in range(5):
        depth, width = (384, 256) if group < 4 else (256, 128)
        total = None
        for q in range(3):
            at = q * 1280 + group * 256
            part = dot(h1[:, at : at + depth], wm[q, :depth, :width])
            total = part if total is None else total + part
        h2[:, group * 256 : group * 256 + width] = jnp.maximum(total, 0.0).astype(BF16)
    acc[...] = dot(h2[...], w3[...])
    noise_t = acc[0:256, 0:128] + acc[1:257, 128:256] + acc[2:258, 256:384]
    return jnp.transpose(noise_t)[:C]


def whiten(detrended, table_hi, table_lo):
    hi = detrended.astype(BF16)
    lo = (detrended - hi.astype(F32)).astype(BF16)
    spec = dot(hi, table_hi[...]) + (dot(lo, table_hi[...]) + dot(hi, table_lo[...]))
    re, im = spec[:, :F], spec[:, F:]
    power = re * re + im * im
    lane = lax.broadcasted_iota(jnp.int32, (C, F), 1)
    smooth = power
    for by in range(1, BAND + 1):
        smooth = smooth + jnp.where(lane >= by, pltpu.roll(power, by, axis=1), 0.0)
        smooth = smooth + jnp.where(lane < F - by, pltpu.roll(power, F - by, axis=1), 0.0)
    mean = jnp.sum(power, axis=1, keepdims=True) * (1.0 / F)
    divisor = jnp.sqrt(smooth * (1.0 / (2 * BAND + 1)) + 0.1 * mean + 1e-6)
    return jnp.concatenate([re / divisor, im / divisor], axis=1).astype(BF16)


def kernel(
    dims, raw_at, first_at, mid_at, last_at, lower_at, upper_at, valid_at, dft_at, lag_at, out,
    raw, w_first, w_mid, w_last, lower, upper, valid, dft, lag, in_sem,
    masked, packet, zbuf, edge_out, edge_in, xsend, xbuf, own_l, own_r,
    w1f, w1, wm, w3, ext, shifted, h1, h2, acc, spec, xall, xf, mine, got, gf, lhs,
    z_send, z_recv, e_send, e_recv, x_send, x_recv, h_send, h_recv, y_send, y_recv, o_send, o_recv,
    r_send, r_recv, n1_send, n1_recv, n2_send, n2_recv, b_send, b_recv,
):
    n_chan, n_seg, n_x = dims
    n_r = n_chan // n_x
    n_z = n_r // 2
    n_y = n_seg // 2
    half = n_chan // 2
    partners = C // n_seg
    rows = C // 2
    chan, seg = lax.axis_index("chan"), lax.axis_index("seg")
    slab = lax.div(chan, n_r)
    place = lax.rem(chan, n_r)
    level = lax.div(place, 2)
    core = lax.rem(place, 2)
    side = lax.div(seg, n_y)
    column = lax.rem(seg, n_y)

    def block_at(k_x, k_z, k_c):
        return (
            lax.rem(slab + k_x, n_x) * n_r + lax.rem(level + k_z, n_z) * 2 + lax.rem(core + k_c, 2)
        )

    def seg_at(k_h, k_y):
        return lax.rem(side + k_h, 2) * n_y + lax.rem(column + k_y, n_y)

    def each(first, last, act):
        def one(k, carry):
            act(k)
            return carry
        lax.fori_loop(first, last, one, 0)

    def send(source, target, sems, at, to):
        return pltpu.make_async_remote_copy(
            source, target, sems[0].at[at], sems[1].at[at], device_id=to, device_id_type=MESH
        )

    arrays = [
        (raw_at, raw), (valid_at, valid), (lower_at, lower), (upper_at, upper), (first_at, w_first),
        (mid_at, w_mid), (last_at, w_last), (dft_at, dft), (lag_at, lag),
    ]
    loads = [pltpu.make_async_copy(a, b, in_sem.at[i]) for i, (a, b) in enumerate(arrays)]
    for load in loads[:4]:
        load.start()

    barrier = pltpu.get_barrier_semaphore()

    def greet(to):
        pl.semaphore_signal(barrier, inc=1, device_id=to, device_id_type=MESH)

    for k_h in range(2):
        each(1 - k_h, n_z, lambda k: greet((block_at(0, k, 0), seg_at(k_h, 0))))
    for step in (1, n_seg - 1):
        each(0, n_z, lambda k: greet((block_at(0, k, 0), lax.rem(seg + step, n_seg))))
    for k in range(1, 2 * n_x):
        greet((block_at(k // 2, 0, k % 2), seg))
    each(1, n_y, lambda k: greet((chan, seg_at(0, k))))
    greeted = (2 * n_z - 1) + 2 * n_z + (2 * n_x - 1) + (n_y - 1)
    for load in loads[4:]:
        load.start()
    for load in loads[:4]:
        load.wait()

    live = (lax.broadcasted_iota(jnp.int32, (C, WIN), 0) < valid[0]).astype(F32)
    own = raw[...].astype(F32) * live
    masked[...] = own.astype(BF16)
    row8 = lax.broadcasted_iota(jnp.int32, (8, WIN), 0)
    goes_low, goes_high = upper[0].astype(F32), lower[0].astype(F32)
    outer = jnp.concatenate([own[13:16], own[0:3], own[0:2]], axis=0)
    outer = jnp.where(row8 == 6, goes_low, jnp.where(row8 == 7, goes_high, outer))
    packet[...] = outer.astype(BF16)
    zbuf[level] = outer.astype(BF16)
    row_t = lax.broadcasted_iota(jnp.int32, (8, 128), 0)
    lane_t = lax.broadcasted_iota(jnp.int32, (8, 128), 1)

    def packed(tile, first):
        out_rows = jnp.zeros((8, 128), F32)
        for r in range(6):
            here = (row_t == r) & (lane_t >= 4 * r) & (lane_t < 4 * r + 3)
            out_rows = jnp.where(here, pltpu.roll(tile, (4 * r - first) % 128, axis=1), out_rows)
        line = jnp.sum(out_rows, axis=0, keepdims=True)
        lane = lax.broadcasted_iota(jnp.int32, (1, 128), 1)
        return jnp.where(lane == 24, goes_low, jnp.where(lane == 25, goes_high, line))

    edge_out[0] = packed(outer[:, 128:256], 125)
    edge_out[1] = packed(outer[:, 0:128], 0)

    pl.semaphore_wait(barrier, greeted)

    def z_copy(k):
        return send(packet, zbuf.at[level], (z_send, z_recv), k, (block_at(0, k, 0), seg))

    def e_copy(way, k):
        step = 1 if way == 0 else n_seg - 1
        to = (block_at(0, k, 0), lax.rem(seg + step, n_seg))
        return send(edge_out.at[way], edge_in.at[way, level], (e_send, e_recv), way * n_z + k, to)

    def x_copy(k):
        return send(xsend.at[k], xbuf.at[k], (x_send, x_recv), k, (block_at(k // 2, 0, k % 2), seg))

    def halo_copy(way):
        source, target, step = [
            (masked.at[:, 128:256], own_l, 1),
            (masked.at[:, 0:128], own_r, n_seg - 1),
        ][way]
        return send(source, target, (h_send, h_recv), way, (chan, lax.rem(seg + step, n_seg)))

    for way in range(2):
        each(0, n_z, lambda k: e_copy(way, k).start())
    each(1, n_z, lambda k: z_copy(k).start())
    for way in range(2):
        halo_copy(way).start()

    for load in loads[4:]:
        load.wait()
    build_weights(w_first, w_mid, w_last, w1f, w1, wm, w3)
    for way in range(2):
        each(0, n_z, lambda k: e_copy(way, k).wait_recv())
    each(1, n_z, lambda k: z_copy(k).wait_recv())
    wanted = [block_at(k // 2, 0, k % 2).astype(F32) for k in range(2 * n_x)]
    picked = [jnp.zeros((8, WIN), F32) for _ in wanted]
    for source in range(n_z):
        values = zbuf[source].astype(F32)
        goes = jnp.where(
            row8 < 3,
            jnp.broadcast_to(values[6:7], (8, WIN)),
            jnp.broadcast_to(values[7:8], (8, WIN)),
        )
        picked = [p + jnp.where(goes == w, values, 0.0) for p, w in zip(picked, wanted)]
    lane_z = lax.broadcasted_iota(jnp.int32, (n_z, 128), 1)
    for way in range(2):
        lines = edge_in[way].reshape(n_z, 128)
        goes = jnp.where(
            lane_z < 12,
            jnp.broadcast_to(lines[:, 24:25], (n_z, 128)),
            jnp.broadcast_to(lines[:, 25:26], (n_z, 128)),
        )
        lines = jnp.where(lane_z < 24, lines, 0.0)
        for k, w in enumerate(wanted):
            line = jnp.sum(jnp.where(goes == w, lines, 0.0), axis=0, keepdims=True)
            line = jnp.concatenate([line, jnp.zeros((1, 128), F32)], axis=1)
            picked[k] = jnp.where(row8 == 6 + way, jnp.broadcast_to(line, (8, WIN)), picked[k])
    for k in range(1, 2 * n_x):
        xsend[k] = picked[k].astype(BF16)
        x_copy(k).start()

    has_before = (seg > 0).astype(F32)
    has_after = (seg < n_seg - 1).astype(F32)
    for way in range(2):
        halo_copy(way).wait_recv()
    lane_c = lax.broadcasted_iota(jnp.int32, (C, 128), 1)
    own_edge = jnp.where(lane_c < 3, own_r[...].astype(F32) * has_after, 0.0)
    own_edge = jnp.where(lane_c >= 125, own_l[...].astype(F32) * has_before, own_edge)
    ext[3:19, 0:256] = own
    ext[3:19, 256:384] = own_edge
    ext[22:24, :] = jnp.zeros((2, 384), F32)
    strips = picked[0]
    for k in range(1, 2 * n_x):
        x_copy(k).wait_recv()
        strips = strips + xbuf[k].astype(F32)
    before = jnp.broadcast_to(strips[6:7, 0:128] * has_before, (8, 128))
    after = jnp.broadcast_to(strips[7:8, 0:128] * has_after, (8, 128))
    strip_edge = jnp.zeros((8, 128), F32)
    for r in range(6):
        late = jnp.where(lane_t >= 125, pltpu.roll(before, 125 - 4 * r, axis=1), 0.0)
        both = jnp.where(lane_t < 3, pltpu.roll(after, (128 - 4 * r) % 128, axis=1), late)
        strip_edge = jnp.where(row_t == r, both, strip_edge)
    ext[0:3, 0:256] = strips[0:3]
    ext[0:3, 256:384] = strip_edge[0:3]
    ext[19:22, 0:256] = strips[3:6]
    ext[19:22, 256:384] = strip_edge[3:6]
    noise = convolve(ext, shifted, w1, wm, w3, h1, h2, acc)
    clean = (own - noise) * live
    common = jnp.sum(clean, axis=0, keepdims=True) / valid[0].astype(F32)
    detrended = (clean - common) * live
    spectra = whiten(detrended, dft.at[0], dft.at[1])
    spec[...] = spectra
    xall[seg] = spectra
    def y_copy(k):
        return send(spec, xall.at[seg], (y_send, y_recv), k, (chan, seg_at(0, k)))

    def across_copy():
        return send(spec, xall.at[seg], (o_send, o_recv), 0, (chan, seg_at(1, 0)))

    def pass_on(k):
        window = xall.at[seg_at(1, 0)]
        return send(window, window, (o_send, o_recv), k, (chan, seg_at(0, k)))

    across_copy().start()
    each(1, n_y, lambda k: y_copy(k).start())
    each(1, n_y, lambda k: y_copy(k).wait_recv())
    flat = xall[pl.ds(side * n_y, n_y)].reshape(n_y * C, 2 * F)
    r_id = lax.broadcasted_iota(jnp.int32, (C, n_y * C), 0)
    c_id = lax.broadcasted_iota(jnp.int32, (C, n_y * C), 1)
    for_seg = (r_id // rows) * n_y + column
    inner = r_id % rows
    source_row = (inner // partners) * C + for_seg * partners + inner % partners
    chosen = dot((c_id == source_row).astype(F32).astype(BF16), flat).astype(BF16)
    mine[...] = chosen.reshape(2, rows, 2 * F)
    got[place, side] = mine[side]

    def r_copy(k_h, k):
        to_side = lax.rem(side + k_h, 2)
        return send(
            mine.at[to_side], got.at[place, side], (r_send, r_recv), k_h * n_z + k,
            (block_at(0, k, 0), seg_at(k_h, 0)),
        )

    order = sorted(range(n_z), key=lambda k: (max(k, n_z - k), k))
    for k in order:
        if k:
            r_copy(0, k).start()
        r_copy(1, k).start()

    def near_copy(at):
        slot = at * 2 + core
        return send(
            got.at[slot], got.at[n_r + slot], (n1_send, n1_recv), at, (block_at(n_x - 1, 0, 0), seg)
        )

    def far_copy(at):
        slot = at * 2 + core
        return send(
            got.at[slot], got.at[2 * n_r + slot], (n2_send, n2_recv), at,
            (block_at(n_x - 2, 0, 0), seg),
        )

    def beside_copy(k_x, at):
        slot = k_x * n_r + at * 2 + core
        return send(
            got.at[slot], got.at[slot], (b_send, b_recv), k_x * n_z + at, (block_at(0, 0, 1), seg)
        )

    for k in order:
        if k:
            r_copy(0, k).wait_recv()
        r_copy(1, k).wait_recv()
        at = lax.rem(level + n_z - k, n_z)
        near_copy(at).start()

        @pl.when(at <= level)
        def _():
            far_copy(at).start()

        @pl.when(at >= level)
        def _():
            beside_copy(0, at).start()

    across_copy().wait_recv()
    each(1, n_y, lambda k: pass_on(k).start())

    for k in order:
        at = lax.rem(level + n_z - k, n_z)
        near_copy(at).wait_recv()
        beside_copy(1, at).start()

        @pl.when(at <= level)
        def _():
            far_copy(at).wait_recv()
            beside_copy(2, at).start()

    each(1, n_y, lambda k: pass_on(k).wait_recv())
    each(level, n_z, lambda at: beside_copy(0, at).wait_recv())
    each(0, n_z, lambda at: beside_copy(1, at).wait_recv())
    each(0, level + 1, lambda at: beside_copy(2, at).wait_recv())
    xf[...] = xall[...].astype(F32)

    def correlate(d):
        gf[...] = got[place + d].astype(F32).reshape(C, 2 * F)
        at = pl.multiple_of(d * C, C)
        for b in range(partners):
            cr = jnp.zeros((C, F), F32)
            ci = jnp.zeros((C, F), F32)
            for w in range(n_seg):
                row = w * partners + b
                pr = jnp.broadcast_to(gf[row : row + 1, 0:F], (C, F))
                pi = jnp.broadcast_to(gf[row : row + 1, F : 2 * F], (C, F))
                ar, ai = xf[w, :, 0:F], xf[w, :, F : 2 * F]
                cr = cr + (ar * pr + ai * pi)
                ci = ci + (ai * pr - ar * pi)
            lhs[pl.ds(at, C), b * 256 : b * 256 + F] = cr
            lhs[pl.ds(at, C), b * 256 + F : b * 256 + 2 * F] = ci

    each(0, half + 1, correlate)
    chunk = next(c for c in range(11, 0, -1) if (half + 1) % c == 0)
    for start in range(0, half + 1, chunk):
        values = lhs[start * C : (start + chunk) * C, :]
        hi = values.astype(BF16)
        lo = (values - hi.astype(F32)).astype(BF16)
        lagged = dot(hi, lag[0]) + (dot(lo, lag[0]) + dot(hi, lag[1]))
        for d in range(chunk):
            out[start + d] = lagged[d * C : (d + 1) * C]

    for way in range(2):
        each(0, n_z, lambda k: e_copy(way, k).wait_send())
        halo_copy(way).wait_send()
    each(1, n_z, lambda k: z_copy(k).wait_send())
    for k in range(1, 2 * n_x):
        x_copy(k).wait_send()
    across_copy().wait_send()
    each(1, n_y, lambda k: y_copy(k).wait_send())
    each(1, n_y, lambda k: pass_on(k).wait_send())
    each(1, n_z, lambda k: r_copy(0, k).wait_send())
    each(0, n_z, lambda k: r_copy(1, k).wait_send())
    each(0, n_z, lambda at: near_copy(at).wait_send())
    each(0, level + 1, lambda at: far_copy(at).wait_send())
    each(level, n_z, lambda at: beside_copy(0, at).wait_send())
    each(0, n_z, lambda at: beside_copy(1, at).wait_send())
    each(0, level + 1, lambda at: beside_copy(2, at).wait_send())


def body(raw, w_first, w_mid, w_last, lower, upper, valid, dims):
    n_chan, n_seg, n_x = dims
    n_r = n_chan // n_x
    n_z = n_r // 2
    n_y = n_seg // 2
    half = n_chan // 2
    partners = C // n_seg
    dft = split_bf16(dft_table())
    lag = split_bf16(lag_table(partners, 1.0 / math.sqrt(n_seg * F)))
    dma = pltpu.SemaphoreType.DMA
    scratch = [
        pltpu.VMEM(raw.shape, BF16),
        pltpu.VMEM(w_first.shape, BF16),
        pltpu.VMEM(w_mid.shape, BF16),
        pltpu.VMEM(w_last.shape, BF16),
        pltpu.SMEM((1,), jnp.int32),
        pltpu.SMEM((1,), jnp.int32),
        pltpu.SMEM((1,), jnp.int32),
        pltpu.VMEM(dft.shape, BF16),
        pltpu.VMEM(lag.shape, BF16),
        dma((9,)),
        pltpu.VMEM((C, WIN), BF16),
        pltpu.VMEM((8, WIN), BF16),
        pltpu.VMEM((n_z, 8, WIN), BF16),
        pltpu.VMEM((2, 1, 128), F32),
        pltpu.VMEM((2, n_z, 1, 128), F32),
        pltpu.VMEM((2 * n_x, 8, WIN), BF16),
        pltpu.VMEM((2 * n_x, 8, WIN), BF16),
        pltpu.VMEM((C, 128), BF16),
        pltpu.VMEM((C, 128), BF16),
        pltpu.VMEM((128, 3840), F32),
        pltpu.VMEM((128, 3840), BF16),
        pltpu.VMEM((3, 384, 256), BF16),
        pltpu.VMEM((1152, 384), BF16),
        pltpu.VMEM((24, 384), F32),
        pltpu.VMEM((128, 384), F32),
        pltpu.VMEM((TPAD, 3840), BF16),
        pltpu.VMEM((TPAD, 1152), BF16),
        pltpu.VMEM((TPAD, 384), F32),
        pltpu.VMEM((C, 2 * F), BF16),
        pltpu.VMEM((n_seg, C, 2 * F), BF16),
        pltpu.VMEM((n_seg, C, 2 * F), F32),
        pltpu.VMEM((2, C // 2, 2 * F), BF16),
        pltpu.VMEM((3 * n_r, 2, C // 2, 2 * F), BF16),
        pltpu.VMEM((C, 2 * F), F32),
        pltpu.VMEM(((half + 1) * C, partners * 2 * F), F32),
        dma((n_z,)), dma((n_z,)), dma((2 * n_z,)), dma((2 * n_z,)), dma((2 * n_x,)), dma((2 * n_x,)),
        dma((2,)), dma((2,)), dma((n_y,)), dma((n_y,)), dma((n_y,)), dma((n_y,)),
        dma((2 * n_z,)), dma((2 * n_z,)), dma((n_z,)), dma((n_z,)), dma((n_z,)), dma((n_z,)),
        dma((3 * n_z,)), dma((3 * n_z,)),
    ]
    lagged = pl.pallas_call(
        functools.partial(kernel, dims),
        out_shape=jax.ShapeDtypeStruct((half + 1, C, partners * NLAG), F32),
        in_specs=[pl.BlockSpec(memory_space=pl.ANY)] * 9,
        out_specs=pl.BlockSpec(memory_space=pltpu.VMEM),
        scratch_shapes=scratch,
        compiler_params=pltpu.CompilerParams(
            collective_id=0, has_side_effects=True, vmem_limit_bytes=48 << 20
        ),
    )(raw, w_first, w_mid, w_last, lower, upper, valid, jnp.asarray(dft), jnp.asarray(lag))
    return jnp.transpose(lagged, (1, 0, 2))


def solution(mesh):
    n_chan, n_seg = mesh.shape["chan"], mesh.shape["seg"]
    dims = (n_chan, n_seg, 4)
    return jax.shard_map(
        functools.partial(body, dims=dims),
        mesh=mesh,
        in_specs=(P("chan", "seg"), P(), P(), P(), P("chan"), P("chan"), P("chan")),
        out_specs=P("chan", None, "seg"),
        check_vma=False,
    )
```

time: 71.1 us -> 60.9 us (0.86)
  Pallas kernels: 62.2 us -> 53.7 us
  local copies, waits for them, and re-layouts: 6.66 us -> 4.9 us
    pallas_call x1, Pallas kernels: 62.2 us -> 53.7 us  [body(): pl.pallas_call(functools.partial(kernel, dims), out_shape=jax.ShapeDtypeS...]
    unnamed x16 -> x13, local copies, waits for them, and re-layouts: 5.9 us -> 4.9 us
    pallas_call x1 -> x0, local copies, waits for them, and re-layouts: 0.76 us -> none  [body(): pl.pallas_call(functools.partial(kernel, dims), out_shape=jax.ShapeDtypeS...]
where the time goes in v2:
time: 60.9 us; the launch traced here: 60.6 us
  Pallas kernels  53.7 us (88%)
  local copies, waits for them, and re-layouts  4.9 us (8%)
  between operations  1.98 us (3%)
    pallas_call x1, Pallas kernels, body(): pl.pallas_call(functools.partial(kernel, dims), out_shape=jax.ShapeDtypeS...  53.7 us
    unnamed x13, local copies, waits for them, and re-layouts  4.9 us

profile of v2, /device:TPU:1, one launch (start us, length us, event | category | flops | bytes accessed | tf_op | source)
XLA Modules:
  0.0 60.6 jit_solution(11431403728889341112)
XLA Ops:
  0.0 0.0 copy-start.4
  2.0 0.0 copy-done.4
  2.0 0.0 copy-start
  2.0 0.9 %copy-done = bf16[2,512,128]{2,1,0:T(8,128)(2,1)S(1)} copy-done((bf16[2,512,128]{2,1,0:T(8,128)(2,1)S(1)}, bf16[2,512,128]{2,1,0:T(8,128)(2,1)}, u32[]{:S(2)}) %copy-start) | copy-done | bytes 262168
  2.9 0.0 copy-start.1
  2.9 0.9 %copy-done.1 = bf16[2,256,256]{2,1,0:T(8,128)(2,1)S(1)} copy-done((bf16[2,256,256]{2,1,0:T(8,128)(2,1)S(1)}, bf16[2,256,256]{2,1,0:T(8,128)(2,1)}, u32[]{:S(2)}) %copy-start.1) | copy-done | bytes 262168
  3.9 0.0 copy-start.2
  3.9 0.9 %copy-done.2 = bf16[1,9,64,64]{3,2,1,0:T(8,128)(2,1)S(1)} copy-done((bf16[1,9,64,64]{3,2,1,0:T(8,128)(2,1)S(1)}, bf16[1,9,64,64]{3,2,1,0:T(8,128)(2,1)}, u32[]{:S(2)}) %copy-start.2) | copy-done | bytes 73752
  4.8 0.0 copy-start.3
  4.8 0.7 %copy-done.3 = bf16[16,256]{1,0:T(8,128)(2,1)S(1)} copy-done((bf16[16,256]{1,0:T(8,128)(2,1)S(1)}, bf16[16,256]{1,0:T(8,128)(2,1)}, u32[]{:S(2)}) %copy-start.3) | copy-done | bytes 8216
  5.5 0.0 copy-start.5
  5.5 0.7 %copy-done.5 = bf16[9,64]{1,0:T(8,128)(2,1)S(1)} copy-done((bf16[9,64]{1,0:T(8,128)(2,1)S(1)}, bf16[9,64]{1,0:T(8,128)(2,1)}, u32[]{:S(2)}) %copy-start.5) | copy-done | bytes 1176
  6.2 53.7 %shard_map.91 = f32[33,16,128]{2,1,0:T(8,128)S(1)} custom-call(bf16[16,256]{1,0:T(8,128)(2,1)S(1)} %copy-done.3, bf16[9,64]{1,0:T(8,128)(2,1)S(1)} %copy-done.4, bf16[1,9,64,64]{3,2,1,0:T(8,128)(2,1)S(1)} %copy-done.2, bf16[9,64]{1,0:T(8,128)(2,1)S(1)} %copy-done.5, s32[1]{0:T(128)S(6)} %copy.11.lower_at, s32[1]{0:T(128)S(6)} %copy.12.upper_at, ...), custom_call_target="tpu_custom_call" | custom-call | tf_op jit(solution)/shard_map/pallas_call | solution.py:482
  59.9 0.7 %copy.14 = f32[16,33,128]{2,0,1:T(8,128)} copy(f32[16,33,128]{2,0,1:T(8,128)S(1)} %bitcast.1) | data formatting | bytes 540672
Async XLA Ops:
  0.0 2.0 %copy-start.4 = (bf16[9,64]{1,0:T(8,128)(2,1)S(1)}, bf16[9,64]{1,0:T(8,128)(2,1)}, u32[]{:S(2)}) copy-start(bf16[9,64]{1,0:T(8,128)(2,1)} %first_at.1) | copy-start | bytes 3460
  2.0 1.0 %copy-start = (bf16[2,512,128]{2,1,0:T(8,128)(2,1)S(1)}, bf16[2,512,128]{2,1,0:T(8,128)(2,1)}, u32[]{:S(2)}) copy-start(bf16[2,512,128]{2,1,0:T(8,128)(2,1)} %constant.5.clone.lag_at) | copy-start | bytes 786436
  2.9 0.9 %copy-start.1 = (bf16[2,256,256]{2,1,0:T(8,128)(2,1)S(1)}, bf16[2,256,256]{2,1,0:T(8,128)(2,1)}, u32[]{:S(2)}) copy-start(bf16[2,256,256]{2,1,0:T(8,128)(2,1)} %constant.4.clone.dft_at) | copy-start | bytes 786436
  3.9 0.9 %copy-start.2 = (bf16[1,9,64,64]{3,2,1,0:T(8,128)(2,1)S(1)}, bf16[1,9,64,64]{3,2,1,0:T(8,128)(2,1)}, u32[]{:S(2)}) copy-start(bf16[1,9,64,64]{3,2,1,0:T(8,128)(2,1)} %mid_at.1) | copy-start | bytes 221188
  4.8 0.7 %copy-start.3 = (bf16[16,256]{1,0:T(8,128)(2,1)S(1)}, bf16[16,256]{1,0:T(8,128)(2,1)}, u32[]{:S(2)}) copy-start(bf16[16,256]{1,0:T(8,128)(2,1)} %raw_at.1) | copy-start | bytes 24580
  5.5 0.7 %copy-start.5 = (bf16[9,64]{1,0:T(8,128)(2,1)S(1)}, bf16[9,64]{1,0:T(8,128)(2,1)}, u32[]{:S(2)}) copy-start(bf16[9,64]{1,0:T(8,128)(2,1)} %last_at.1) | copy-start | bytes 3460

commit v3 on v2

--- a/solution.py
+++ b/solution.py
@@ -109,12 +109,12 @@
         smooth = smooth + jnp.where(lane < F - by, pltpu.roll(power, F - by, axis=1), 0.0)
     mean = jnp.sum(power, axis=1, keepdims=True) * (1.0 / F)
     divisor = jnp.sqrt(smooth * (1.0 / (2 * BAND + 1)) + 0.1 * mean + 1e-6)
-    return jnp.concatenate([re / divisor, im / divisor], axis=1).astype(BF16)
+    return jnp.concatenate([re / divisor, im / divisor], axis=1)
 
 
 def kernel(
-    dims, raw_at, first_at, mid_at, last_at, lower_at, upper_at, valid_at, dft_at, lag_at, out,
-    raw, w_first, w_mid, w_last, lower, upper, valid, dft, lag, in_sem,
+    dims, raw_at, first_at, mid_at, last_at, lower, upper, valid, dft_at, lag_at, out,
+    raw, w_first, w_mid, w_last, dft, lag, in_sem,
     masked, packet, zbuf, edge_out, edge_in, xsend, xbuf, own_l, own_r,
     w1f, w1, wm, w3, ext, shifted, h1, h2, acc, spec, xall, xf, mine, got, gf, lhs,
     z_send, z_recv, e_send, e_recv, x_send, x_recv, h_send, h_recv, y_send, y_recv, o_send, o_recv,
@@ -126,7 +126,6 @@
     n_y = n_seg // 2
     half = n_chan // 2
     partners = C // n_seg
-    rows = C // 2
     chan, seg = lax.axis_index("chan"), lax.axis_index("seg")
     slab = lax.div(chan, n_r)
     place = lax.rem(chan, n_r)
@@ -155,11 +154,11 @@
         )
 
     arrays = [
-        (raw_at, raw), (valid_at, valid), (lower_at, lower), (upper_at, upper), (first_at, w_first),
+        (raw_at, raw), (first_at, w_first),
         (mid_at, w_mid), (last_at, w_last), (dft_at, dft), (lag_at, lag),
     ]
     loads = [pltpu.make_async_copy(a, b, in_sem.at[i]) for i, (a, b) in enumerate(arrays)]
-    for load in loads[:4]:
+    for load in loads[:1]:
         load.start()
 
     barrier = pltpu.get_barrier_semaphore()
@@ -175,9 +174,9 @@
         greet((block_at(k // 2, 0, k % 2), seg))
     each(1, n_y, lambda k: greet((chan, seg_at(0, k))))
     greeted = (2 * n_z - 1) + 2 * n_z + (2 * n_x - 1) + (n_y - 1)
-    for load in loads[4:]:
+    for load in loads[1:]:
         load.start()
-    for load in loads[:4]:
+    for load in loads[:1]:
         load.wait()
 
     live = (lax.broadcasted_iota(jnp.int32, (C, WIN), 0) < valid[0]).astype(F32)
@@ -230,7 +229,7 @@
     for way in range(2):
         halo_copy(way).start()
 
-    for load in loads[4:]:
+    for load in loads[1:]:
         load.wait()
     build_weights(w_first, w_mid, w_last, w1f, w1, wm, w3)
     for way in range(2):
@@ -293,8 +292,10 @@
     common = jnp.sum(clean, axis=0, keepdims=True) / valid[0].astype(F32)
     detrended = (clean - common) * live
     spectra = whiten(detrended, dft.at[0], dft.at[1])
-    spec[...] = spectra
-    xall[seg] = spectra
+    for to in range(n_seg):
+        mine[to] = spectra[to * partners : (to + 1) * partners].astype(BF16)
+    spec[...] = spectra.astype(BF16)
+    xall[seg] = spectra.astype(BF16)
     def y_copy(k):
         return send(spec, xall.at[seg], (y_send, y_recv), k, (chan, seg_at(0, k)))
 
@@ -305,32 +306,20 @@
         window = xall.at[seg_at(1, 0)]
         return send(window, window, (o_send, o_recv), k, (chan, seg_at(0, k)))
 
+    got[place, seg] = mine[seg]
+
+    def r_copy(k_s, k):
+        to_seg = lax.rem(seg + k_s, n_seg)
+        return send(
+            mine.at[to_seg], got.at[place, seg], (r_send, r_recv), k_s * n_z + k,
+            (block_at(0, k, 0), to_seg),
+        )
+
+    order = sorted(range(n_z), key=lambda k: (max(k, n_z - k), k))
+    for k in reversed(order):
+        each(0 if k else 1, n_seg, lambda k_s: r_copy(k_s, k).start())
     across_copy().start()
     each(1, n_y, lambda k: y_copy(k).start())
-    each(1, n_y, lambda k: y_copy(k).wait_recv())
-    flat = xall[pl.ds(side * n_y, n_y)].reshape(n_y * C, 2 * F)
-    r_id = lax.broadcasted_iota(jnp.int32, (C, n_y * C), 0)
-    c_id = lax.broadcasted_iota(jnp.int32, (C, n_y * C), 1)
-    for_seg = (r_id // rows) * n_y + column
-    inner = r_id % rows
-    source_row = (inner // partners) * C + for_seg * partners + inner % partners
-    chosen = dot((c_id == source_row).astype(F32).astype(BF16), flat).astype(BF16)
-    mine[...] = chosen.reshape(2, rows, 2 * F)
-    got[place, side] = mine[side]
-
-    def r_copy(k_h, k):
-        to_side = lax.rem(side + k_h, 2)
-        return send(
-            mine.at[to_side], got.at[place, side], (r_send, r_recv), k_h * n_z + k,
-            (block_at(0, k, 0), seg_at(k_h, 0)),
-        )
-
-    order = sorted(range(n_z), key=lambda k: (max(k, n_z - k), k))
-    for k in order:
-        if k:
-            r_copy(0, k).start()
-        r_copy(1, k).start()
-
     def near_copy(at):
         slot = at * 2 + core
         return send(
@@ -350,10 +339,18 @@
             got.at[slot], got.at[slot], (b_send, b_recv), k_x * n_z + at, (block_at(0, 0, 1), seg)
         )
 
+    def other_needs(k_x, at):
+        first = level * 2 + 1 - core
+        slot = k_x * n_r + at * 2 + core
+        return (slot >= first) & (slot <= first + half)
+
+    def beside(k_x, at, act):
+        @pl.when(other_needs(k_x, at))
+        def _():
+            act(beside_copy(k_x, at))
+
     for k in order:
-        if k:
-            r_copy(0, k).wait_recv()
-        r_copy(1, k).wait_recv()
+        each(0 if k else 1, n_seg, lambda k_s: r_copy(k_s, k).wait_recv())
         at = lax.rem(level + n_z - k, n_z)
         near_copy(at).start()
 
@@ -361,31 +358,35 @@
         def _():
             far_copy(at).start()
 
-        @pl.when(at >= level)
-        def _():
-            beside_copy(0, at).start()
-
+        beside(0, at, lambda copy: copy.start())
     across_copy().wait_recv()
     each(1, n_y, lambda k: pass_on(k).start())
 
     for k in order:
         at = lax.rem(level + n_z - k, n_z)
         near_copy(at).wait_recv()
-        beside_copy(1, at).start()
+        beside(1, at, lambda copy: copy.start())
 
         @pl.when(at <= level)
         def _():
             far_copy(at).wait_recv()
-            beside_copy(2, at).start()
-
+
+        beside(2, at, lambda copy: copy.start())
+
+    each(1, n_y, lambda k: y_copy(k).wait_recv())
     each(1, n_y, lambda k: pass_on(k).wait_recv())
-    each(level, n_z, lambda at: beside_copy(0, at).wait_recv())
-    each(0, n_z, lambda at: beside_copy(1, at).wait_recv())
-    each(0, level + 1, lambda at: beside_copy(2, at).wait_recv())
     xf[...] = xall[...].astype(F32)
-
     def correlate(d):
-        gf[...] = got[place + d].astype(F32).reshape(C, 2 * F)
+        slot = place + d
+
+        @pl.when(lax.rem(slot, 2) != core)
+        def _():
+            k_x = lax.div(slot, n_r)
+            at = lax.div(lax.rem(slot, n_r), 2)
+            beside_copy(k_x, at).wait_recv()
+
+        for w in range(n_seg):
+            gf[w * partners : (w + 1) * partners, :] = got[slot, w].astype(F32)
         at = pl.multiple_of(d * C, C)
         for b in range(partners):
             cr = jnp.zeros((C, F), F32)
@@ -400,9 +401,9 @@
             lhs[pl.ds(at, C), b * 256 : b * 256 + F] = cr
             lhs[pl.ds(at, C), b * 256 + F : b * 256 + 2 * F] = ci
 
-    each(0, half + 1, correlate)
     chunk = next(c for c in range(11, 0, -1) if (half + 1) % c == 0)
     for start in range(0, half + 1, chunk):
+        each(start, start + chunk, correlate)
         values = lhs[start * C : (start + chunk) * C, :]
         hi = values.astype(BF16)
         lo = (values - hi.astype(F32)).astype(BF16)
@@ -419,13 +420,12 @@
     across_copy().wait_send()
     each(1, n_y, lambda k: y_copy(k).wait_send())
     each(1, n_y, lambda k: pass_on(k).wait_send())
-    each(1, n_z, lambda k: r_copy(0, k).wait_send())
-    each(0, n_z, lambda k: r_copy(1, k).wait_send())
+    for k in range(n_z):
+        each(0 if k else 1, n_seg, lambda k_s: r_copy(k_s, k).wait_send())
     each(0, n_z, lambda at: near_copy(at).wait_send())
     each(0, level + 1, lambda at: far_copy(at).wait_send())
-    each(level, n_z, lambda at: beside_copy(0, at).wait_send())
-    each(0, n_z, lambda at: beside_copy(1, at).wait_send())
-    each(0, level + 1, lambda at: beside_copy(2, at).wait_send())
+    for k_x in range(3):
+        each(0, n_z, lambda at: beside(k_x, at, lambda copy: copy.wait_send()))
 
 
 def body(raw, w_first, w_mid, w_last, lower, upper, valid, dims):
@@ -443,12 +443,9 @@
         pltpu.VMEM(w_first.shape, BF16),
         pltpu.VMEM(w_mid.shape, BF16),
         pltpu.VMEM(w_last.shape, BF16),
-        pltpu.SMEM((1,), jnp.int32),
-        pltpu.SMEM((1,), jnp.int32),
-        pltpu.SMEM((1,), jnp.int32),
         pltpu.VMEM(dft.shape, BF16),
         pltpu.VMEM(lag.shape, BF16),
-        dma((9,)),
+        dma((6,)),
         pltpu.VMEM((C, WIN), BF16),
         pltpu.VMEM((8, WIN), BF16),
         pltpu.VMEM((n_z, 8, WIN), BF16),
@@ -470,23 +467,25 @@
         pltpu.VMEM((C, 2 * F), BF16),
         pltpu.VMEM((n_seg, C, 2 * F), BF16),
         pltpu.VMEM((n_seg, C, 2 * F), F32),
-        pltpu.VMEM((2, C // 2, 2 * F), BF16),
-        pltpu.VMEM((3 * n_r, 2, C // 2, 2 * F), BF16),
+        pltpu.VMEM((n_seg, partners, 2 * F), BF16),
+        pltpu.VMEM((3 * n_r, n_seg, partners, 2 * F), BF16),
         pltpu.VMEM((C, 2 * F), F32),
         pltpu.VMEM(((half + 1) * C, partners * 2 * F), F32),
         dma((n_z,)), dma((n_z,)), dma((2 * n_z,)), dma((2 * n_z,)), dma((2 * n_x,)), dma((2 * n_x,)),
         dma((2,)), dma((2,)), dma((n_y,)), dma((n_y,)), dma((n_y,)), dma((n_y,)),
-        dma((2 * n_z,)), dma((2 * n_z,)), dma((n_z,)), dma((n_z,)), dma((n_z,)), dma((n_z,)),
+        dma((n_seg * n_z,)), dma((n_seg * n_z,)), dma((n_z,)), dma((n_z,)), dma((n_z,)), dma((n_z,)),
         dma((3 * n_z,)), dma((3 * n_z,)),
     ]
+    hbm = pl.BlockSpec(memory_space=pltpu.HBM)
+    smem = pl.BlockSpec(memory_space=pltpu.SMEM)
     lagged = pl.pallas_call(
         functools.partial(kernel, dims),
         out_shape=jax.ShapeDtypeStruct((half + 1, C, partners * NLAG), F32),
-        in_specs=[pl.BlockSpec(memory_space=pl.ANY)] * 9,
+        in_specs=[hbm] * 4 + [smem] * 3 + [hbm] * 2,
         out_specs=pl.BlockSpec(memory_space=pltpu.VMEM),
         scratch_shapes=scratch,
         compiler_params=pltpu.CompilerParams(
-            collective_id=0, has_side_effects=True, vmem_limit_bytes=48 << 20
+            collective_id=0, has_side_effects=True, vmem_limit_bytes=60 << 20
         ),
     )(raw, w_first, w_mid, w_last, lower, upper, valid, jnp.asarray(dft), jnp.asarray(lag))
     return jnp.transpose(lagged, (1, 0, 2))

time: 60.9 us -> 56.5 us (0.928)
  local copies, waits for them, and re-layouts: 4.9 us -> 1.68 us
  Pallas kernels: 53.7 us -> 52.7 us
    unnamed x13 -> x1, local copies, waits for them, and re-layouts: 4.9 us -> 1.68 us
    pallas_call x1, Pallas kernels: 53.7 us -> 52.7 us  [body(): pl.pallas_call(functools.partial(kernel, dims), out_shape=jax.ShapeDtypeS...]
where the time goes in v3:
time: 56.5 us; the launch traced here: 56.3 us
  Pallas kernels  52.7 us (93%)
  between operations  1.95 us (3%)
  local copies, waits for them, and re-layouts  1.68 us (3%)
    pallas_call x1, Pallas kernels, body(): pl.pallas_call(functools.partial(kernel, dims), out_shape=jax.ShapeDtypeS...  52.7 us
    unnamed x1, local copies, waits for them, and re-layouts  1.68 us

profile of v3, /device:TPU:1, one launch (start us, length us, event | category | flops | bytes accessed | tf_op | source)
XLA Modules:
  0.0 56.3 jit_solution(7781279322866405172)
XLA Ops:
  1.9 52.7 %shard_map.91 = f32[33,16,128]{2,1,0:T(8,128)} custom-call(bf16[16,256]{1,0:T(8,128)(2,1)} %raw_at.1, bf16[9,64]{1,0:T(8,128)(2,1)} %first_at.1, bf16[1,9,64,64]{3,2,1,0:T(8,128)(2,1)} %mid_at.1, bf16[9,64]{1,0:T(8,128)(2,1)} %last_at.1, s32[1]{0:T(128)S(6)} %copy.11.lower, s32[1]{0:T(128)S(6)} %copy.12.upper, s32[1]{0:T(128)S(6)} %copy.13.valid, ...), custom_call_target="tpu_custom_call" | custom-call | tf_op jit(solution)/shard_map/pallas_call | solution.py:481
  54.6 1.7 %copy.14 = f32[16,33,128]{2,0,1:T(8,128)} copy(f32[16,33,128]{2,0,1:T(8,128)} %bitcast.1) | data formatting | bytes 540672

commit v4 on v3

--- a/solution.py
+++ b/solution.py
@@ -116,7 +116,7 @@
     dims, raw_at, first_at, mid_at, last_at, lower, upper, valid, dft_at, lag_at, out,
     raw, w_first, w_mid, w_last, dft, lag, in_sem,
     masked, packet, zbuf, edge_out, edge_in, xsend, xbuf, own_l, own_r,
-    w1f, w1, wm, w3, ext, shifted, h1, h2, acc, spec, xall, xf, mine, got, gf, lhs,
+    w1f, w1, wm, w3, ext, shifted, h1, h2, acc, spec, xall, xf, mine, got, gf, lhs, result, out_sem,
     z_send, z_recv, e_send, e_recv, x_send, x_recv, h_send, h_recv, y_send, y_recv, o_send, o_recv,
     r_send, r_recv, n1_send, n1_recv, n2_send, n2_recv, b_send, b_recv,
 ):
@@ -149,9 +149,16 @@
         lax.fori_loop(first, last, one, 0)
 
     def send(source, target, sems, at, to):
+        if at is None:
+            sent, landed = (sem.at[i] for sem, i in sems)
+        else:
+            sent, landed = (sem.at[at] for sem in sems)
         return pltpu.make_async_remote_copy(
-            source, target, sems[0].at[at], sems[1].at[at], device_id=to, device_id_type=MESH
-        )
+            source, target, sent, landed, device_id=to, device_id_type=MESH
+        )
+
+    def all_of(ref, sem):
+        pltpu.make_async_copy(ref, ref, sem).wait()
 
     arrays = [
         (raw_at, raw), (first_at, w_first),
@@ -206,15 +213,15 @@
     pl.semaphore_wait(barrier, greeted)
 
     def z_copy(k):
-        return send(packet, zbuf.at[level], (z_send, z_recv), k, (block_at(0, k, 0), seg))
+        return send(packet, zbuf.at[level], (z_send, z_recv), 0, (block_at(0, k, 0), seg))
 
     def e_copy(way, k):
         step = 1 if way == 0 else n_seg - 1
         to = (block_at(0, k, 0), lax.rem(seg + step, n_seg))
-        return send(edge_out.at[way], edge_in.at[way, level], (e_send, e_recv), way * n_z + k, to)
+        return send(edge_out.at[way], edge_in.at[way, level], (e_send, e_recv), way, to)
 
     def x_copy(k):
-        return send(xsend.at[k], xbuf.at[k], (x_send, x_recv), k, (block_at(k // 2, 0, k % 2), seg))
+        return send(xsend.at[k], xbuf.at[k], (x_send, x_recv), 0, (block_at(k // 2, 0, k % 2), seg))
 
     def halo_copy(way):
         source, target, step = [
@@ -233,8 +240,8 @@
         load.wait()
     build_weights(w_first, w_mid, w_last, w1f, w1, wm, w3)
     for way in range(2):
-        each(0, n_z, lambda k: e_copy(way, k).wait_recv())
-    each(1, n_z, lambda k: z_copy(k).wait_recv())
+        all_of(edge_in.at[way], e_recv.at[way])
+    all_of(zbuf.at[0 : n_z - 1], z_recv.at[0])
     wanted = [block_at(k // 2, 0, k % 2).astype(F32) for k in range(2 * n_x)]
     picked = [jnp.zeros((8, WIN), F32) for _ in wanted]
     for source in range(n_z):
@@ -273,8 +280,8 @@
     ext[3:19, 256:384] = own_edge
     ext[22:24, :] = jnp.zeros((2, 384), F32)
     strips = picked[0]
+    all_of(xbuf.at[1 : 2 * n_x], x_recv.at[0])
     for k in range(1, 2 * n_x):
-        x_copy(k).wait_recv()
         strips = strips + xbuf[k].astype(F32)
     before = jnp.broadcast_to(strips[6:7, 0:128] * has_before, (8, 128))
     after = jnp.broadcast_to(strips[7:8, 0:128] * has_after, (8, 128))
@@ -297,21 +304,21 @@
     spec[...] = spectra.astype(BF16)
     xall[seg] = spectra.astype(BF16)
     def y_copy(k):
-        return send(spec, xall.at[seg], (y_send, y_recv), k, (chan, seg_at(0, k)))
+        return send(spec, xall.at[seg], (y_send, y_recv), 0, (chan, seg_at(0, k)))
 
     def across_copy():
         return send(spec, xall.at[seg], (o_send, o_recv), 0, (chan, seg_at(1, 0)))
 
     def pass_on(k):
         window = xall.at[seg_at(1, 0)]
-        return send(window, window, (o_send, o_recv), k, (chan, seg_at(0, k)))
+        return send(window, window, (o_send, o_recv), 1, (chan, seg_at(0, k)))
 
     got[place, seg] = mine[seg]
 
     def r_copy(k_s, k):
         to_seg = lax.rem(seg + k_s, n_seg)
         return send(
-            mine.at[to_seg], got.at[place, seg], (r_send, r_recv), k_s * n_z + k,
+            mine.at[to_seg], got.at[place, seg], (r_send, r_recv), k,
             (block_at(0, k, 0), to_seg),
         )
 
@@ -323,20 +330,21 @@
     def near_copy(at):
         slot = at * 2 + core
         return send(
-            got.at[slot], got.at[n_r + slot], (n1_send, n1_recv), at, (block_at(n_x - 1, 0, 0), seg)
+            got.at[slot], got.at[n_r + slot], ((n1_send, 0), (n1_recv, at)), None, (block_at(n_x - 1, 0, 0), seg)
         )
 
     def far_copy(at):
         slot = at * 2 + core
         return send(
-            got.at[slot], got.at[2 * n_r + slot], (n2_send, n2_recv), at,
+            got.at[slot], got.at[2 * n_r + slot], ((n2_send, 0), (n2_recv, at)), None,
             (block_at(n_x - 2, 0, 0), seg),
         )
 
     def beside_copy(k_x, at):
         slot = k_x * n_r + at * 2 + core
         return send(
-            got.at[slot], got.at[slot], (b_send, b_recv), k_x * n_z + at, (block_at(0, 0, 1), seg)
+            got.at[slot], got.at[slot], ((b_send, k_x), (b_recv, k_x * n_z + at)), None,
+            (block_at(0, 0, 1), seg),
         )
 
     def other_needs(k_x, at):
@@ -350,8 +358,9 @@
             act(beside_copy(k_x, at))
 
     for k in order:
-        each(0 if k else 1, n_seg, lambda k_s: r_copy(k_s, k).wait_recv())
         at = lax.rem(level + n_z - k, n_z)
+        whole = got.at[at * 2 + core]
+        all_of(whole if k else got.at[place, 0 : n_seg - 1], r_recv.at[k])
         near_copy(at).start()
 
         @pl.when(at <= level)
@@ -373,8 +382,9 @@
 
         beside(2, at, lambda copy: copy.start())
 
-    each(1, n_y, lambda k: y_copy(k).wait_recv())
-    each(1, n_y, lambda k: pass_on(k).wait_recv())
+    if n_y > 1:
+        all_of(xall.at[0 : n_y - 1], y_recv.at[0])
+        all_of(xall.at[0 : n_y - 1], o_recv.at[1])
     xf[...] = xall[...].astype(F32)
     def correlate(d):
         slot = place + d
@@ -401,6 +411,7 @@
             lhs[pl.ds(at, C), b * 256 : b * 256 + F] = cr
             lhs[pl.ds(at, C), b * 256 + F : b * 256 + 2 * F] = ci
 
+    stores = []
     chunk = next(c for c in range(11, 0, -1) if (half + 1) % c == 0)
     for start in range(0, half + 1, chunk):
         each(start, start + chunk, correlate)
@@ -409,23 +420,30 @@
         lo = (values - hi.astype(F32)).astype(BF16)
         lagged = dot(hi, lag[0]) + (dot(lo, lag[0]) + dot(hi, lag[1]))
         for d in range(chunk):
-            out[start + d] = lagged[d * C : (d + 1) * C]
+            result[start + d] = lagged[d * C : (d + 1) * C]
+        part = pl.ds(start, chunk)
+        stores.append(
+            pltpu.make_async_copy(result.at[part], out.at[part], out_sem.at[len(stores)])
+        )
+        stores[-1].start()
 
     for way in range(2):
-        each(0, n_z, lambda k: e_copy(way, k).wait_send())
+        all_of(edge_in.at[way], e_send.at[way])
         halo_copy(way).wait_send()
-    each(1, n_z, lambda k: z_copy(k).wait_send())
-    for k in range(1, 2 * n_x):
-        x_copy(k).wait_send()
+    all_of(zbuf.at[0 : n_z - 1], z_send.at[0])
+    all_of(xsend.at[1 : 2 * n_x], x_send.at[0])
     across_copy().wait_send()
-    each(1, n_y, lambda k: y_copy(k).wait_send())
-    each(1, n_y, lambda k: pass_on(k).wait_send())
+    if n_y > 1:
+        all_of(xall.at[0 : n_y - 1], y_send.at[0])
+        all_of(xall.at[0 : n_y - 1], o_send.at[1])
     for k in range(n_z):
-        each(0 if k else 1, n_seg, lambda k_s: r_copy(k_s, k).wait_send())
-    each(0, n_z, lambda at: near_copy(at).wait_send())
+        all_of(mine if k else mine.at[0 : n_seg - 1], r_send.at[k])
+    all_of(got.at[0:n_z], n1_send.at[0])
     each(0, level + 1, lambda at: far_copy(at).wait_send())
     for k_x in range(3):
         each(0, n_z, lambda at: beside(k_x, at, lambda copy: copy.wait_send()))
+    for store in stores:
+        store.wait()
 
 
 def body(raw, w_first, w_mid, w_last, lower, upper, valid, dims):
@@ -438,6 +456,8 @@
     dft = split_bf16(dft_table())
     lag = split_bf16(lag_table(partners, 1.0 / math.sqrt(n_seg * F)))
     dma = pltpu.SemaphoreType.DMA
+    chunk = next(c for c in range(11, 0, -1) if (half + 1) % c == 0)
+    chunks = (half + 1) // chunk
     scratch = [
         pltpu.VMEM(raw.shape, BF16),
         pltpu.VMEM(w_first.shape, BF16),
@@ -471,10 +491,12 @@
         pltpu.VMEM((3 * n_r, n_seg, partners, 2 * F), BF16),
         pltpu.VMEM((C, 2 * F), F32),
         pltpu.VMEM(((half + 1) * C, partners * 2 * F), F32),
-        dma((n_z,)), dma((n_z,)), dma((2 * n_z,)), dma((2 * n_z,)), dma((2 * n_x,)), dma((2 * n_x,)),
-        dma((2,)), dma((2,)), dma((n_y,)), dma((n_y,)), dma((n_y,)), dma((n_y,)),
-        dma((n_seg * n_z,)), dma((n_seg * n_z,)), dma((n_z,)), dma((n_z,)), dma((n_z,)), dma((n_z,)),
-        dma((3 * n_z,)), dma((3 * n_z,)),
+        pltpu.VMEM((half + 1, C, partners * NLAG), F32),
+        dma((chunks,)),
+        dma((1,)), dma((1,)), dma((2,)), dma((2,)), dma((1,)), dma((1,)),
+        dma((2,)), dma((2,)), dma((1,)), dma((1,)), dma((2,)), dma((2,)),
+        dma((n_z,)), dma((n_z,)), dma((1,)), dma((n_z,)), dma((1,)), dma((n_z,)),
+        dma((3,)), dma((3 * n_z,)),
     ]
     hbm = pl.BlockSpec(memory_space=pltpu.HBM)
     smem = pl.BlockSpec(memory_space=pltpu.SMEM)
@@ -482,7 +504,7 @@
         functools.partial(kernel, dims),
         out_shape=jax.ShapeDtypeStruct((half + 1, C, partners * NLAG), F32),
         in_specs=[hbm] * 4 + [smem] * 3 + [hbm] * 2,
-        out_specs=pl.BlockSpec(memory_space=pltpu.VMEM),
+        out_specs=hbm,
         scratch_shapes=scratch,
         compiler_params=pltpu.CompilerParams(
             collective_id=0, has_side_effects=True, vmem_limit_bytes=60 << 20

time: 56.5 us -> 53.5 us (0.947)
  Pallas kernels: 52.7 us -> 49.7 us
    pallas_call x1, Pallas kernels: 52.7 us -> 49.7 us  [body(): pl.pallas_call(functools.partial(kernel, dims), out_shape=jax.ShapeDtypeS...]
where the time goes in v4:
time: 53.5 us; the launch traced here: 53.3 us
  Pallas kernels  49.7 us (93%)
  between operations  1.95 us (4%)
  local copies, waits for them, and re-layouts  1.68 us (3%)
    pallas_call x1, Pallas kernels, body(): pl.pallas_call(functools.partial(kernel, dims), out_shape=jax.ShapeDtypeS...  49.7 us
    unnamed x1, local copies, waits for them, and re-layouts  1.68 us

profile of v4, /device:TPU:1, one launch (start us, length us, event | category | flops | bytes accessed | tf_op | source)
XLA Modules:
  0.0 53.3 jit_solution(2862359628106229121)
XLA Ops:
  1.9 49.7 %shard_map.91 = f32[33,16,128]{2,1,0:T(8,128)} custom-call(bf16[16,256]{1,0:T(8,128)(2,1)} %raw_at.1, bf16[9,64]{1,0:T(8,128)(2,1)} %first_at.1, bf16[1,9,64,64]{3,2,1,0:T(8,128)(2,1)} %mid_at.1, bf16[9,64]{1,0:T(8,128)(2,1)} %last_at.1, s32[1]{0:T(128)S(6)} %copy.11.lower, s32[1]{0:T(128)S(6)} %copy.12.upper, s32[1]{0:T(128)S(6)} %copy.13.valid, ...), custom_call_target="tpu_custom_call" | custom-call | tf_op jit(solution)/shard_map/pallas_call | solution.py:503
  51.6 1.7 %copy.14 = f32[16,33,128]{2,0,1:T(8,128)} copy(f32[16,33,128]{2,0,1:T(8,128)} %bitcast.1) | data formatting | bytes 540672

commit v5 on v4

--- a/solution.py
+++ b/solution.py
@@ -116,7 +116,7 @@
     dims, raw_at, first_at, mid_at, last_at, lower, upper, valid, dft_at, lag_at, out,
     raw, w_first, w_mid, w_last, dft, lag, in_sem,
     masked, packet, zbuf, edge_out, edge_in, xsend, xbuf, own_l, own_r,
-    w1f, w1, wm, w3, ext, shifted, h1, h2, acc, spec, xall, xf, mine, got, gf, lhs, result, out_sem,
+    w1f, w1, wm, w3, ext, shifted, h1, h2, acc, spec, xall, xf, mine, got, gf, lhs,
     z_send, z_recv, e_send, e_recv, x_send, x_recv, h_send, h_recv, y_send, y_recv, o_send, o_recv,
     r_send, r_recv, n1_send, n1_recv, n2_send, n2_recv, b_send, b_recv,
 ):
@@ -318,7 +318,7 @@
     def r_copy(k_s, k):
         to_seg = lax.rem(seg + k_s, n_seg)
         return send(
-            mine.at[to_seg], got.at[place, seg], (r_send, r_recv), k,
+            mine.at[to_seg], got.at[place, seg], ((r_send, 0), (r_recv, k)), None,
             (block_at(0, k, 0), to_seg),
         )
 
@@ -343,7 +343,7 @@
     def beside_copy(k_x, at):
         slot = k_x * n_r + at * 2 + core
         return send(
-            got.at[slot], got.at[slot], ((b_send, k_x), (b_recv, k_x * n_z + at)), None,
+            got.at[slot], got.at[slot], ((b_send, 0), (b_recv, k_x * n_z + at)), None,
             (block_at(0, 0, 1), seg),
         )
 
@@ -411,7 +411,6 @@
             lhs[pl.ds(at, C), b * 256 : b * 256 + F] = cr
             lhs[pl.ds(at, C), b * 256 + F : b * 256 + 2 * F] = ci
 
-    stores = []
     chunk = next(c for c in range(11, 0, -1) if (half + 1) % c == 0)
     for start in range(0, half + 1, chunk):
         each(start, start + chunk, correlate)
@@ -420,12 +419,7 @@
         lo = (values - hi.astype(F32)).astype(BF16)
         lagged = dot(hi, lag[0]) + (dot(lo, lag[0]) + dot(hi, lag[1]))
         for d in range(chunk):
-            result[start + d] = lagged[d * C : (d + 1) * C]
-        part = pl.ds(start, chunk)
-        stores.append(
-            pltpu.make_async_copy(result.at[part], out.at[part], out_sem.at[len(stores)])
-        )
-        stores[-1].start()
+            out[start + d] = lagged[d * C : (d + 1) * C]
 
     for way in range(2):
         all_of(edge_in.at[way], e_send.at[way])
@@ -437,13 +431,11 @@
         all_of(xall.at[0 : n_y - 1], y_send.at[0])
         all_of(xall.at[0 : n_y - 1], o_send.at[1])
     for k in range(n_z):
-        all_of(mine if k else mine.at[0 : n_seg - 1], r_send.at[k])
+        all_of(mine if k else mine.at[0 : n_seg - 1], r_send.at[0])
     all_of(got.at[0:n_z], n1_send.at[0])
     each(0, level + 1, lambda at: far_copy(at).wait_send())
     for k_x in range(3):
         each(0, n_z, lambda at: beside(k_x, at, lambda copy: copy.wait_send()))
-    for store in stores:
-        store.wait()
 
 
 def body(raw, w_first, w_mid, w_last, lower, upper, valid, dims):
@@ -456,8 +448,6 @@
     dft = split_bf16(dft_table())
     lag = split_bf16(lag_table(partners, 1.0 / math.sqrt(n_seg * F)))
     dma = pltpu.SemaphoreType.DMA
-    chunk = next(c for c in range(11, 0, -1) if (half + 1) % c == 0)
-    chunks = (half + 1) // chunk
     scratch = [
         pltpu.VMEM(raw.shape, BF16),
         pltpu.VMEM(w_first.shape, BF16),
@@ -491,25 +481,27 @@
         pltpu.VMEM((3 * n_r, n_seg, partners, 2 * F), BF16),
         pltpu.VMEM((C, 2 * F), F32),
         pltpu.VMEM(((half + 1) * C, partners * 2 * F), F32),
-        pltpu.VMEM((half + 1, C, partners * NLAG), F32),
-        dma((chunks,)),
         dma((1,)), dma((1,)), dma((2,)), dma((2,)), dma((1,)), dma((1,)),
         dma((2,)), dma((2,)), dma((1,)), dma((1,)), dma((2,)), dma((2,)),
-        dma((n_z,)), dma((n_z,)), dma((1,)), dma((n_z,)), dma((1,)), dma((n_z,)),
-        dma((3,)), dma((3 * n_z,)),
+        dma((1,)), dma((n_z,)), dma((1,)), dma((n_z,)), dma((1,)), dma((n_z,)),
+        dma((1,)), dma((3 * n_z,)),
     ]
     hbm = pl.BlockSpec(memory_space=pltpu.HBM)
     smem = pl.BlockSpec(memory_space=pltpu.SMEM)
+    placed = [raw, w_first, w_mid, w_last, lower, upper, valid, jnp.asarray(dft), jnp.asarray(lag)]
+    placed = [
+        x if x.ndim == 1 else pltpu.with_memory_space_constraint(x, pltpu.HBM) for x in placed
+    ]
     lagged = pl.pallas_call(
         functools.partial(kernel, dims),
         out_shape=jax.ShapeDtypeStruct((half + 1, C, partners * NLAG), F32),
         in_specs=[hbm] * 4 + [smem] * 3 + [hbm] * 2,
-        out_specs=hbm,
+        out_specs=pl.BlockSpec(memory_space=pltpu.VMEM),
         scratch_shapes=scratch,
         compiler_params=pltpu.CompilerParams(
-            collective_id=0, has_side_effects=True, vmem_limit_bytes=60 << 20
+            collective_id=0, has_side_effects=True, vmem_limit_bytes=48 << 20
         ),
-    )(raw, w_first, w_mid, w_last, lower, upper, valid, jnp.asarray(dft), jnp.asarray(lag))
+    )(*placed)
     return jnp.transpose(lagged, (1, 0, 2))
 
 

time: 53.5 us -> 52 us (0.972)
  local copies, waits for them, and re-layouts: 1.68 us -> 0.71 us
    unnamed x1, local copies, waits for them, and re-layouts: 1.68 us -> 0.71 us
where the time goes in v5:
time: 52 us; the launch traced here: 51.9 us
  Pallas kernels  49.2 us (95%)
  between operations  1.95 us (4%)
  local copies, waits for them, and re-layouts  0.71 us (1%)
    pallas_call x1, Pallas kernels, body(): pl.pallas_call(functools.partial(kernel, dims), out_shape=jax.ShapeDtypeS...  49.2 us

profile of v5, /device:TPU:1, one launch (start us, length us, event | category | flops | bytes accessed | tf_op | source)
XLA Modules:
  0.0 51.9 jit_solution(17371345955546215728)
XLA Ops:
  1.9 49.2 %shard_map.91 = f32[33,16,128]{2,1,0:T(8,128)S(1)} custom-call(bf16[16,256]{1,0:T(8,128)(2,1)} %raw_at.1, bf16[9,64]{1,0:T(8,128)(2,1)} %first_at.1, bf16[1,9,64,64]{3,2,1,0:T(8,128)(2,1)} %mid_at.1, bf16[9,64]{1,0:T(8,128)(2,1)} %last_at.1, s32[1]{0:T(128)S(6)} %copy.11.lower, s32[1]{0:T(128)S(6)} %copy.12.upper, s32[1]{0:T(128)S(6)} %copy.13.valid, ...), custom_call_target="tpu_custom_call" | custom-call | tf_op jit(solution)/shard_map/pallas_call | solution.py:495
  51.2 0.7 %copy.14 = f32[16,33,128]{2,0,1:T(8,128)} copy(f32[16,33,128]{2,0,1:T(8,128)S(1)} %bitcast.1) | data formatting | bytes 540672

commit v6 on v5

--- a/solution.py
+++ b/solution.py
@@ -74,16 +74,17 @@
             w3[row * 64 : (row + 1) * 64, q * 128 : (q + 1) * 128] = rolled.astype(BF16)
 
 
-def convolve(ext, shifted, w1, wm, w3, h1, h2, acc):
+def hide(ext, shifted, w1, wm, h1, h2, groups, ready):
     whole = ext[...]
     for q in range(5):
         shifted[q * 24 : (q + 1) * 24, :] = pltpu.roll(whole, (3 - q) % 384, axis=1)
     shifted[120:128, :] = jnp.zeros((8, 384), F32)
     patches = jnp.transpose(shifted[...])[:TPAD].astype(BF16)
-    for block in range(15):
-        cols = slice(block * 256, (block + 1) * 256)
-        h1[:, cols] = jnp.maximum(dot(patches, w1[:, cols]), 0.0).astype(BF16)
-    for group in range(5):
+    for group in groups:
+        for late in range(3):
+            at = late * 1280 + group * 256
+            h1[:, at : at + 256] = jnp.maximum(dot(patches, w1[:, at : at + 256]), 0.0).astype(BF16)
+    for group in ready:
         depth, width = (384, 256) if group < 4 else (256, 128)
         total = None
         for q in range(3):
@@ -91,9 +92,6 @@
             part = dot(h1[:, at : at + depth], wm[q, :depth, :width])
             total = part if total is None else total + part
         h2[:, group * 256 : group * 256 + width] = jnp.maximum(total, 0.0).astype(BF16)
-    acc[...] = dot(h2[...], w3[...])
-    noise_t = acc[0:256, 0:128] + acc[1:257, 128:256] + acc[2:258, 256:384]
-    return jnp.transpose(noise_t)[:C]
 
 
 def whiten(detrended, table_hi, table_lo):
@@ -173,10 +171,10 @@
     def greet(to):
         pl.semaphore_signal(barrier, inc=1, device_id=to, device_id_type=MESH)
 
+    for step in (1, n_seg - 1):
+        each(0, n_z, lambda k: greet((block_at(0, k, 0), lax.rem(seg + step, n_seg))))
     for k_h in range(2):
         each(1 - k_h, n_z, lambda k: greet((block_at(0, k, 0), seg_at(k_h, 0))))
-    for step in (1, n_seg - 1):
-        each(0, n_z, lambda k: greet((block_at(0, k, 0), lax.rem(seg + step, n_seg))))
     for k in range(1, 2 * n_x):
         greet((block_at(k // 2, 0, k % 2), seg))
     each(1, n_y, lambda k: greet((chan, seg_at(0, k))))
@@ -278,7 +276,10 @@
     own_edge = jnp.where(lane_c >= 125, own_l[...].astype(F32) * has_before, own_edge)
     ext[3:19, 0:256] = own
     ext[3:19, 256:384] = own_edge
-    ext[22:24, :] = jnp.zeros((2, 384), F32)
+    ext[0:3, :] = jnp.zeros((3, 384), F32)
+    ext[19:24, :] = jnp.zeros((5, 384), F32)
+    hide(ext, shifted, w1, wm, h1, h2, (1, 2, 3), (1, 2))
+    acc[...] = dot(h2[:, 256:768], w3[256:768])
     strips = picked[0]
     all_of(xbuf.at[1 : 2 * n_x], x_recv.at[0])
     for k in range(1, 2 * n_x):
@@ -294,7 +295,10 @@
     ext[0:3, 256:384] = strip_edge[0:3]
     ext[19:22, 0:256] = strips[3:6]
     ext[19:22, 256:384] = strip_edge[3:6]
-    noise = convolve(ext, shifted, w1, wm, w3, h1, h2, acc)
+    hide(ext, shifted, w1, wm, h1, h2, (0, 4), (0, 3, 4))
+    acc[...] += dot(h2[:, 0:256], w3[0:256]) + dot(h2[:, 768:1152], w3[768:1152])
+    noise_t = acc[0:256, 0:128] + acc[1:257, 128:256] + acc[2:258, 256:384]
+    noise = jnp.transpose(noise_t)[:C]
     clean = (own - noise) * live
     common = jnp.sum(clean, axis=0, keepdims=True) / valid[0].astype(F32)
     detrended = (clean - common) * live
@@ -322,29 +326,23 @@
             (block_at(0, k, 0), to_seg),
         )
 
+    across_copy().start()
+    each(1, n_y, lambda k: y_copy(k).start())
     order = sorted(range(n_z), key=lambda k: (max(k, n_z - k), k))
     for k in reversed(order):
         each(0 if k else 1, n_seg, lambda k_s: r_copy(k_s, k).start())
-    across_copy().start()
-    each(1, n_y, lambda k: y_copy(k).start())
-    def near_copy(at):
+    def slab_copy(k_x, at, k_c):
+        slot = at * 2 + core
+        sent, landed = (n1_send, n1_recv) if k_x == 1 else (n2_send, n2_recv)
+        return send(
+            got.at[slot], got.at[k_x * n_r + slot], ((sent, 0), (landed, k_c * n_z + at)), None,
+            (block_at(n_x - k_x, 0, k_c), seg),
+        )
+
+    def beside_copy(at):
         slot = at * 2 + core
         return send(
-            got.at[slot], got.at[n_r + slot], ((n1_send, 0), (n1_recv, at)), None, (block_at(n_x - 1, 0, 0), seg)
-        )
-
-    def far_copy(at):
-        slot = at * 2 + core
-        return send(
-            got.at[slot], got.at[2 * n_r + slot], ((n2_send, 0), (n2_recv, at)), None,
-            (block_at(n_x - 2, 0, 0), seg),
-        )
-
-    def beside_copy(k_x, at):
-        slot = k_x * n_r + at * 2 + core
-        return send(
-            got.at[slot], got.at[slot], ((b_send, 0), (b_recv, k_x * n_z + at)), None,
-            (block_at(0, 0, 1), seg),
+            got.at[slot], got.at[slot], ((b_send, 0), (b_recv, at)), None, (block_at(0, 0, 1), seg)
         )
 
     def other_needs(k_x, at):
@@ -352,35 +350,30 @@
         slot = k_x * n_r + at * 2 + core
         return (slot >= first) & (slot <= first + half)
 
-    def beside(k_x, at, act):
-        @pl.when(other_needs(k_x, at))
+    def leaving(at, act):
+        @pl.when(at <= level)
         def _():
-            act(beside_copy(k_x, at))
-
-    for k in order:
+            act(slab_copy(2, at, 0))
+
+        @pl.when(other_needs(2, at))
+        def _():
+            act(slab_copy(2, at, 1))
+
+        for k_c in range(2):
+            act(slab_copy(1, at, k_c))
+
+        @pl.when(other_needs(0, at))
+        def _():
+            act(beside_copy(at))
+
+    for turn, k in enumerate(order):
+        if turn == min(3, n_z - 1):
+            across_copy().wait_recv()
+            each(1, n_y, lambda k: pass_on(k).start())
         at = lax.rem(level + n_z - k, n_z)
         whole = got.at[at * 2 + core]
         all_of(whole if k else got.at[place, 0 : n_seg - 1], r_recv.at[k])
-        near_copy(at).start()
-
-        @pl.when(at <= level)
-        def _():
-            far_copy(at).start()
-
-        beside(0, at, lambda copy: copy.start())
-    across_copy().wait_recv()
-    each(1, n_y, lambda k: pass_on(k).start())
-
-    for k in order:
-        at = lax.rem(level + n_z - k, n_z)
-        near_copy(at).wait_recv()
-        beside(1, at, lambda copy: copy.start())
-
-        @pl.when(at <= level)
-        def _():
-            far_copy(at).wait_recv()
-
-        beside(2, at, lambda copy: copy.start())
+        leaving(at, lambda copy: copy.start())
 
     if n_y > 1:
         all_of(xall.at[0 : n_y - 1], y_recv.at[0])
@@ -389,11 +382,18 @@
     def correlate(d):
         slot = place + d
 
-        @pl.when(lax.rem(slot, 2) != core)
+        k_x, at = lax.div(slot, n_r), lax.div(lax.rem(slot, n_r), 2)
+        apart = lax.rem(slot + core, 2)
+
+        @pl.when((k_x == 0) & (apart == 1))
         def _():
-            k_x = lax.div(slot, n_r)
-            at = lax.div(lax.rem(slot, n_r), 2)
-            beside_copy(k_x, at).wait_recv()
+            beside_copy(at).wait_recv()
+
+        for far, landed in ((1, n1_recv), (2, n2_recv)):
+
+            @pl.when(k_x == far)
+            def _():
+                all_of(got.at[slot], landed.at[apart * n_z + at])
 
         for w in range(n_seg):
             gf[w * partners : (w + 1) * partners, :] = got[slot, w].astype(F32)
@@ -432,10 +432,7 @@
         all_of(xall.at[0 : n_y - 1], o_send.at[1])
     for k in range(n_z):
         all_of(mine if k else mine.at[0 : n_seg - 1], r_send.at[0])
-    all_of(got.at[0:n_z], n1_send.at[0])
-    each(0, level + 1, lambda at: far_copy(at).wait_send())
-    for k_x in range(3):
-        each(0, n_z, lambda at: beside(k_x, at, lambda copy: copy.wait_send()))
+    each(0, n_z, lambda at: leaving(at, lambda copy: copy.wait_send()))
 
 
 def body(raw, w_first, w_mid, w_last, lower, upper, valid, dims):
@@ -483,8 +480,8 @@
         pltpu.VMEM(((half + 1) * C, partners * 2 * F), F32),
         dma((1,)), dma((1,)), dma((2,)), dma((2,)), dma((1,)), dma((1,)),
         dma((2,)), dma((2,)), dma((1,)), dma((1,)), dma((2,)), dma((2,)),
-        dma((1,)), dma((n_z,)), dma((1,)), dma((n_z,)), dma((1,)), dma((n_z,)),
-        dma((1,)), dma((3 * n_z,)),
+        dma((1,)), dma((n_z,)), dma((1,)), dma((2 * n_z,)), dma((1,)), dma((2 * n_z,)),
+        dma((1,)), dma((n_z,)),
     ]
     hbm = pl.BlockSpec(memory_space=pltpu.HBM)
     smem = pl.BlockSpec(memory_space=pltpu.SMEM)

time: 52 us -> 49.6 us (0.954)
  Pallas kernels: 49.2 us -> 46.8 us
    pallas_call x1, Pallas kernels: 49.2 us -> 46.8 us  [body(): pl.pallas_call(functools.partial(kernel, dims), out_shape=jax.ShapeDtypeS...]
where the time goes in v6:
time: 49.6 us; the launch traced here: 49.4 us
  Pallas kernels  46.8 us (94%)
  between operations  1.95 us (4%)
  local copies, waits for them, and re-layouts  0.71 us (1%)
    pallas_call x1, Pallas kernels, body(): pl.pallas_call(functools.partial(kernel, dims), out_shape=jax.ShapeDtypeS...  46.8 us

profile of v6, /device:TPU:1, one launch (start us, length us, event | category | flops | bytes accessed | tf_op | source)
XLA Modules:
  0.0 49.4 jit_solution(7925067550948910290)
XLA Ops:
  1.9 46.8 %shard_map.91 = f32[33,16,128]{2,1,0:T(8,128)S(1)} custom-call(bf16[16,256]{1,0:T(8,128)(2,1)} %raw_at.1, bf16[9,64]{1,0:T(8,128)(2,1)} %first_at.1, bf16[1,9,64,64]{3,2,1,0:T(8,128)(2,1)} %mid_at.1, bf16[9,64]{1,0:T(8,128)(2,1)} %last_at.1, s32[1]{0:T(128)S(6)} %copy.11.lower, s32[1]{0:T(128)S(6)} %copy.12.upper, s32[1]{0:T(128)S(6)} %copy.13.valid, ...), custom_call_target="tpu_custom_call" | custom-call | tf_op jit(solution)/shard_map/pallas_call | solution.py:492
  48.7 0.7 %copy.14 = f32[16,33,128]{2,0,1:T(8,128)} copy(f32[16,33,128]{2,0,1:T(8,128)S(1)} %bitcast.1) | data formatting | bytes 540672

commit v7 on v6

--- a/solution.py
+++ b/solution.py
@@ -230,7 +230,8 @@
 
     for way in range(2):
         each(0, n_z, lambda k: e_copy(way, k).start())
-    each(1, n_z, lambda k: z_copy(k).start())
+    for k in sorted(range(1, n_z), key=lambda k: -min(k, n_z - k)):
+        z_copy(k).start()
     for way in range(2):
         halo_copy(way).start()
 
@@ -351,6 +352,9 @@
         return (slot >= first) & (slot <= first + half)
 
     def leaving(at, act):
+        for k_c in range(2):
+            act(slab_copy(1, at, k_c))
+
         @pl.when(at <= level)
         def _():
             act(slab_copy(2, at, 0))
@@ -358,9 +362,6 @@
         @pl.when(other_needs(2, at))
         def _():
             act(slab_copy(2, at, 1))
-
-        for k_c in range(2):
-            act(slab_copy(1, at, k_c))
 
         @pl.when(other_needs(0, at))
         def _():

time: 49.6 us -> 49.1 us (0.990)
  Pallas kernels: 46.8 us -> 46.3 us
    pallas_call x1, Pallas kernels: 46.8 us -> 46.3 us  [body(): pl.pallas_call(functools.partial(kernel, dims), out_shape=jax.ShapeDtypeS...]
where the time goes in v7:
time: 49.1 us; the launch traced here: 48.9 us
  Pallas kernels  46.3 us (94%)
  between operations  1.95 us (4%)
  local copies, waits for them, and re-layouts  0.71 us (1%)
    pallas_call x1, Pallas kernels, body(): pl.pallas_call(functools.partial(kernel, dims), out_shape=jax.ShapeDtypeS...  46.3 us

profile of v7, /device:TPU:1, one launch (start us, length us, event | category | flops | bytes accessed | tf_op | source)
XLA Modules:
  0.0 48.9 jit_solution(4716047159576476603)
XLA Ops:
  1.9 46.3 %shard_map.91 = f32[33,16,128]{2,1,0:T(8,128)S(1)} custom-call(bf16[16,256]{1,0:T(8,128)(2,1)} %raw_at.1, bf16[9,64]{1,0:T(8,128)(2,1)} %first_at.1, bf16[1,9,64,64]{3,2,1,0:T(8,128)(2,1)} %mid_at.1, bf16[9,64]{1,0:T(8,128)(2,1)} %last_at.1, s32[1]{0:T(128)S(6)} %copy.11.lower, s32[1]{0:T(128)S(6)} %copy.12.upper, s32[1]{0:T(128)S(6)} %copy.13.valid, ...), custom_call_target="tpu_custom_call" | custom-call | tf_op jit(solution)/shard_map/pallas_call | solution.py:493
  48.2 0.7 %copy.14 = f32[16,33,128]{2,0,1:T(8,128)} copy(f32[16,33,128]{2,0,1:T(8,128)S(1)} %bitcast.1) | data formatting | bytes 540672
